TPU v7x, 32 devices: a whole 2x2x4 slice. The times are simulated.
32 devices in a mesh: space: 16 (over z, x, core), chan: 2 (over y).
Axes of the slice: x: 2, y: 2, z: 4, core: 2. Of those that a mesh axis runs over, the one named last changes fastest.
Arguments:
- patches: bfloat16 [16, 4096, 1024], P('chan', 'space'), may hold values from -6 to 6
- var_embed: float32 [16, 1024], P('chan'), may hold values from -3 to 3
- agg_query: float32 [1024], replicated, may hold values from -18 to 18
- pos_embed: bfloat16 [4096, 1024], P('space'), may hold values from -3 to 3
- gain_first: float32 [1024], replicated, may hold values from 0.1 to 1.9
- gain_second: float32 [1024], replicated, may hold values from 0.1 to 1.9
- w_qkv: bfloat16 [1024, 3, 1024], P(None, None, 'chan'), may hold values from -0.3 to 0.3
- w_out: bfloat16 [1024, 1024], P('chan'), may hold values from -0.1875 to 0.1875
- w_dec: bfloat16 [1024, 1024], replicated, may hold values from -0.1875 to 0.1875
- mod_scale: float32 [16, 1024], P('chan'), may hold values from -3 to 3
- mod_shift: float32 [16, 1024], P('chan'), may hold values from -3 to 3
Outputs:
- decoded: bfloat16 [16, 4096, 1024], P('chan', 'space')
All inputs are finite; a program needn't handle non-finite values.
Results may differ from a plain program's by a relative error of at most 0.025.
Values may be sent and summed in bfloat16 or wider, within the bound.
A program may use at most 64 MiB of HBM per device.

v0:
```python
import math

import jax
import jax.numpy as jnp
from jax import lax
from jax.sharding import PartitionSpec as P

D = 1024
HEADS = 16


epsilon = 1e-06


def merged(array, axis, combine):
    everything = jax.tree.map(
        lambda part, kind: lax.all_gather(part.astype(kind), axis),
        array,
        (jnp.bfloat16, jnp.bfloat16, jnp.bfloat16),
    )

    def take(k):
        return jax.tree.map(lambda part, own: part[k].astype(own.dtype), everything, array)

    return lax.fori_loop(
        1, lax.axis_size(axis), lambda k, so_far: combine(so_far, take(k)), take(0)
    )


def rms_norm(values, gain_vec):
    return values * lax.rsqrt(jnp.mean(values * values, -1, keepdims=True) + epsilon) * gain_vec


def pool_combine(first, second):
    max_one, sum_one, acc_one = first
    max_two, sum_two, acc_two = second
    top_value = jnp.maximum(max_one, max_two)
    left_factor = jnp.exp(max_one - top_value)
    right_factor = jnp.exp(max_two - top_value)
    return (
        top_value,
        sum_one * left_factor + sum_two * right_factor,
        acc_one * left_factor[:, None] + acc_two * right_factor[:, None],
    )


def body(
    patches,
    var_embed,
    agg_query,
    pos_embed,
    gain_first,
    gain_second,
    w_qkv,
    w_out,
    w_dec,
    mod_scale,
    mod_shift,
):
    var_count = patches.shape[0]
    pos_rows = patches.shape[1]
    d_model = patches.shape[2]
    share_cols = d_model // lax.axis_size("chan")
    start_col = lax.axis_index("chan") * share_cols
    embedded = patches.astype(jnp.float32) + var_embed[:, None, :]
    logits = jnp.sum(embedded * agg_query, -1) * (1.0 / math.sqrt(D))
    local_top = jnp.max(logits, 0)
    expo_terms = jnp.exp(logits - local_top)
    part_sum = jnp.sum(expo_terms, 0)
    part_acc = jnp.sum(expo_terms[:, :, None] * embedded, 0)
    _, denom_sum, pooled_acc = merged((local_top, part_sum, part_acc), "chan", pool_combine)
    resid = pooled_acc / denom_sum[:, None] + pos_embed.astype(jnp.float32)
    normed = rms_norm(resid, gain_first).astype(jnp.bfloat16)
    columns = w_qkv.shape[2]
    qkv_all = jnp.dot(
        normed, w_qkv.reshape(d_model, 3 * columns), preferred_element_type=jnp.float32
    ).astype(jnp.bfloat16)
    head_dim = D // HEADS
    head_count = columns // head_dim
    queries = qkv_all[:, :columns].reshape(pos_rows, head_count, head_dim)
    keys_mine = qkv_all[:, columns : 2 * columns]
    values_mine = qkv_all[:, 2 * columns :]
    inv_scale = 1.0 / math.sqrt(head_dim)

    def attend_block(carry, key_block, value_block):
        run_max, run_sum, run_acc = carry
        scores = (
            jnp.einsum("phd,rhd->hpr", queries, key_block, preferred_element_type=jnp.float32)
            * inv_scale
        )
        new_max = jnp.maximum(run_max, jnp.max(scores, -1))
        rescale = jnp.exp(run_max - new_max)
        weights = jnp.exp(scores - new_max[..., None])
        run_sum = run_sum * rescale + jnp.sum(weights, -1)
        run_acc = run_acc * rescale[..., None] + jnp.einsum(
            "hpr,rhd->hpd",
            weights.astype(jnp.bfloat16),
            value_block,
            preferred_element_type=jnp.float32,
        )
        return (new_max, run_sum, run_acc)

    start_state = (
        jnp.full((head_count, pos_rows), -1e30, jnp.float32),
        jnp.zeros((head_count, pos_rows), jnp.float32),
        jnp.zeros((head_count, pos_rows, head_dim), jnp.float32),
    )
    key_piece = lax.all_gather(keys_mine, "space", axis=0, tiled=True)
    value_piece = lax.all_gather(values_mine, "space", axis=0, tiled=True)
    count_rows = key_piece.shape[0]
    key_heads = key_piece.reshape(count_rows, head_count, head_dim)
    value_heads = value_piece.reshape(count_rows, head_count, head_dim)
    blocks = count_rows // 1024
    key_stack = key_heads.reshape(blocks, 1024, head_count, head_dim)
    value_stack = value_heads.reshape(blocks, 1024, head_count, head_dim)

    def step_block(state, pair_in):
        return (attend_block(state, pair_in[0], pair_in[1]), None)

    result, _ = lax.scan(step_block, start_state, (key_stack, value_stack))
    run_max, run_sum, run_acc = result
    mixed = (
        (run_acc / run_sum[..., None])
        .transpose(1, 0, 2)
        .reshape(pos_rows, columns)
        .astype(jnp.bfloat16)
    )
    partial_out = jnp.dot(mixed, w_out, preferred_element_type=jnp.float32)
    share = lax.psum_scatter(
        partial_out.astype(jnp.bfloat16), "chan", scatter_dimension=1, tiled=True
    ).astype(jnp.float32)
    trunk_part = lax.dynamic_slice_in_dim(resid, start_col, share_cols, 1) + share
    square_sum = lax.psum(jnp.sum(trunk_part * trunk_part, 1), "chan")
    gain_part = lax.dynamic_slice_in_dim(gain_second, start_col, share_cols, 0)
    normed_part = (
        trunk_part * lax.rsqrt(square_sum[:, None] / d_model + epsilon) * gain_part
    ).astype(jnp.bfloat16)
    normed_two = lax.all_gather(normed_part, "chan", axis=1, tiled=True)
    modulated = (
        normed_two.astype(jnp.float32)[None] * (1.0 + mod_scale[:, None, :]) + mod_shift[:, None, :]
    ).astype(jnp.bfloat16)
    decoded = jnp.dot(
        modulated.reshape(var_count * pos_rows, d_model), w_dec, preferred_element_type=jnp.float32
    )
    return decoded.reshape(var_count, pos_rows, d_model).astype(jnp.bfloat16)


def solution(mesh):
    placed = (
        P("chan", "space", None),
        P("chan", None),
        P(),
        P("space", None),
        P(),
        P(),
        P(None, None, "chan"),
        P("chan", None),
        P(),
        P("chan", None),
        P("chan", None),
    )
    return jax.shard_map(
        body, mesh=mesh, in_specs=placed, out_specs=P("chan", "space", None), check_vma=False
    )
```

profile of v0, /device:TPU:11, one launch (start us, length us, event | category | flops | bytes accessed | tf_op | source)
XLA Modules:
  0.0 264.6 jit_solution(2596732728070033116)
XLA Ops:
  6.5 0.0 copy-start
  6.5 0.0 copy-start.3
  6.5 0.0 copy-start.7
  6.5 0.0 all-gather.13.cloned.1.call-start
  6.5 3.5 %multiply_reduce_fusion.1 = f32[8,256]{1,0:T(8,128)S(1)} fusion(bf16[8,256,1024]{2,1,0:T(8,128)(2,1)} %param.13, f32[1024]{0:T(1024)} %param.15, f32[8,1024]{1,0:T(8,128)} %param.14), kind=kLoop, calls=%fused_computation.24 | loop fusion | flops 8386560 | bytes 4239360 | tf_op jit(solution)/shard_map/reduce_sum | solution.py:66
  10.1 3.8 %multiply_reduce_fusion = bf16[256,1024]{1,0:T(8,128)(2,1)} fusion(bf16[8,256,1024]{2,1,0:T(8,128)(2,1)} %param.13, f32[8,256]{1,0:T(8,128)S(1)} %get-tuple-element.136, f32[8,1024]{1,0:T(8,128)} %param.14), kind=kLoop, calls=%fused_computation.23 | loop fusion | flops 8126464 | bytes 4759552 | tf_op jit(solution)/shard_map/reduce_sum | solution.py:70
  13.9 0.0 all-gather.13.cloned.1.call-update
  14.0 0.0 all-gather.9.cloned.1.call-start
  14.0 4.6 %copy.24 = bf16[1024,3,512]{0,2,1:T(8,128)(2,1)} copy(bf16[1024,3,512]{2,0,1:T(8,128)(2,1)} %param.19) | data formatting | bytes 6291456 | tf_op args[6]
  18.7 3.1 %all-gather.4 = bf16[2,1,256]{2,1,0:T(2,128)(2,1)S(1)} all-gather(bf16[1,1,256]{2,1,0:T(2,128)(2,1)S(1)} %reshape.160), channel_id=4, replica_groups=mesh['space'=16,'chan'=2] {'chan'}, dimensions={0}, use_global_device_ids=true | all-gather | bytes 1536 | tf_op jit(solution)/shard_map/all_gather | solution.py:17
  21.8 3.1 %all-gather.3 = bf16[2,1,256]{2,1,0:T(2,128)(2,1)S(1)} all-gather(bf16[1,1,256]{2,1,0:T(2,128)(2,1)S(1)} %reshape.158), channel_id=3, replica_groups=mesh['space'=16,'chan'=2] {'chan'}, dimensions={0}, use_global_device_ids=true | all-gather | bytes 1536 | tf_op jit(solution)/shard_map/all_gather | solution.py:17
  24.9 11.5 %all-gather.13.cloned.1.call-done = bf16[512,1024]{1,0:T(8,128)(2,1)} async-done(((bf16[256,1024]{1,0:T(8,128)(2,1)}), bf16[512,1024]{1,0:T(8,128)(2,1)}) %all-gather.13.cloned.1.call-update) | async-done | bytes 1048592 | tf_op jit(solution)/shard_map/all_gather | solution.py:17
  36.4 0.0 copy-done.3
  36.4 1.7 multiply_reduce_fusion.2
  38.1 0.0 copy-start.2
  38.1 1.0 copy-done.2
  39.1 0.0 copy-done.7
  39.1 2.9 %convolution_convert_fusion = bf16[256,1536]{1,0:T(8,128)(2,1)S(1)} fusion(bf16[1024,1536]{0,1:T(8,128)(2,1)} %bitcast.49, f32[256,1024]{1,0:T(8,128)S(1)} %get-tuple-element.131, f32[1024]{0:T(1024)S(1)} %copy-done.7, f32[256]{0:T(256)S(1)} %add_rsqrt_fusion.1), kind=kOutput, calls=%fused_computation.31 | convolution fusion | flops 806486016 | bytes 4985856 | tf_op jit(solution)/shard_map/dot_general | solution.py:75
  42.0 0.9 fusion.36
  42.9 0.0 all-gather.9.cloned.1.call-update
  42.9 0.0 all-gather.11.cloned.1.call-start
  43.0 0.7 all-gather.11.cloned.1.call-update
  43.6 0.2 reduce-scatter.2.cloned.1.call-start
  43.9 0.1 copy.26
  44.0 49.1 %all-gather.9.cloned.1.call-done = bf16[4096,512]{1,0:T(8,128)(2,1)} async-done(((bf16[256,512]{1,0:T(8,128)(2,1)}), bf16[4096,512]{1,0:T(8,128)(2,1)}) %all-gather.9.cloned.1.call-update) | async-done | bytes 4194320 | tf_op jit(solution)/shard_map/all_gather | solution.py:108
  93.1 11.2 %reshape.171 = bf16[4,1024,8,64]{3,2,1,0:T(8,128)(2,1)} reshape(bf16[4096,512]{1,0:T(8,128)(2,1)} %all-gather.9.cloned.1.call-done) | data formatting | bytes 8388608 | tf_op jit(solution)/shard_map/reshape;reshape | solution.py:114
  104.3 9.8 %copy.28 = bf16[4,1024,8,64]{1,3,2,0:T(8,128)(2,1)} copy(bf16[4,1024,8,64]{3,2,1,0:T(8,128)(2,1)} %reshape.171) | data formatting | bytes 8388608
  114.1 30.2 %all-gather.11.cloned.1.call-done = bf16[4096,512]{1,0:T(8,128)(2,1)} async-done(((bf16[256,512]{1,0:T(8,128)(2,1)}), bf16[4096,512]{1,0:T(8,128)(2,1)}) %all-gather.11.cloned.1.call-update) | async-done | bytes 4194320 | tf_op jit(solution)/shard_map/all_gather | solution.py:109
  144.3 11.2 %reshape.172 = bf16[4,1024,8,64]{3,2,1,0:T(8,128)(2,1)} reshape(bf16[4096,512]{1,0:T(8,128)(2,1)} %all-gather.11.cloned.1.call-done) | data formatting | bytes 8388608 | tf_op jit(solution)/shard_map/reshape;reshape | solution.py:115
  155.5 9.8 %copy.29 = bf16[4,1024,8,64]{1,3,2,0:T(8,128)(2,1)} copy(bf16[4,1024,8,64]{3,2,1,0:T(8,128)(2,1)} %reshape.172) | data formatting | bytes 8388608
  165.2 0.0 copy-start.4
  165.2 0.0 copy-start.6
  165.2 57.6 %while.3 = (s32[]{:T(128)}, f32[8,256]{1,0:T(8,128)S(1)}, f32[8,256]{1,0:T(8,128)S(1)}, f32[8,256,64]{1,2,0:T(8,128)S(1)}, bf16[4,1024,8,64]{1,3,2,0:T(8,128)(2,...) while((s32[]{:T(128)}, f32[8,256]{1,0:T(8,128)S(1)}, ...), condition=%wide.region_8.0_spmd.clone, body=%wide.region_5.8_spmd.clone.sunk | while | flops 554051584 | bytes 62260356 | solution.py:120
  165.2 5.8 %bitcast_reduce_fusion.2 = (f32[8,256]{1,0:T(8,128)S(1)}, f32[8,1024,256]{2,1,0:T(8,128)}) fusion(bf16[256,8,64]{0,2,1:T(8,128)(2,1)S(1)} %get-tuple-element.220, bf16[4,1024,8,64]{1,3,2,0:T(8,128)(2,1)} %get-tuple-element.219, s32[]{:T(128)} %get-tuple-element.206), kind=kOutput, calls=%fused_computation.1.clone.1 | convolution fusion | flops 272627712 | bytes 9708032 | tf_op jit(solution)/shard_map/while/body/eval_jaxpr/phd,rhd->hpr/dot_general | solution.py:88
  171.0 4.9 %fusion.50 = f32[8,256]{1,0:T(8,128)S(1)} fusion(f32[8,1024,256]{2,1,0:T(8,128)} %get-tuple-element.194, f32[8,256]{1,0:T(8,128)S(1)} %select_maximum_fusion.2), kind=kLoop, calls=%fused_computation.4.clone.1 | loop fusion | flops 6289408 | bytes 8404992 | tf_op jit(solution)/shard_map/while/body/eval_jaxpr/reduce_sum | solution.py:94
  176.0 0.8 copy-done.1
  176.8 2.8 %fusion.52 = f32[8,256,64]{1,2,0:T(8,128)S(1)} fusion(f32[8,1024,256]{2,1,0:T(8,128)S(1)} %copy-done.1, f32[8,256]{1,0:T(8,128)S(1)} %select_maximum_fusion.2, bf16[4,1024,8,64]{1,3,2,0:T(8,128)(2,1)} %get-tuple-element.221, s32[]{:T(128)} %get-tuple-element.206, f32[8,256,64]{1,2,0:T(8,128)S(1)} %get-tuple-element.209, ...), kind=kOutput, calls=%fused_computation.8.clone.1 | convolution fusion | flops 275120128 | bytes 10502657 | tf_op jit(solution)/shard_map/while/body/eval_jaxpr/hpr,rhd->hpd/dot_general | solution.py:95
  179.6 5.8 %bitcast_reduce_fusion.2 = (f32[8,256]{1,0:T(8,128)S(1)}, f32[8,1024,256]{2,1,0:T(8,128)}) fusion(bf16[256,8,64]{0,2,1:T(8,128)(2,1)S(1)} %get-tuple-element.220, bf16[4,1024,8,64]{1,3,2,0:T(8,128)(2,1)} %get-tuple-element.219, s32[]{:T(128)} %get-tuple-element.206), kind=kOutput, calls=%fused_computation.1.clone.1 | convolution fusion | flops 272627712 | bytes 9708032 | tf_op jit(solution)/shard_map/while/body/eval_jaxpr/phd,rhd->hpr/dot_general | solution.py:88
  185.4 4.9 %fusion.50 = f32[8,256]{1,0:T(8,128)S(1)} fusion(f32[8,1024,256]{2,1,0:T(8,128)} %get-tuple-element.194, f32[8,256]{1,0:T(8,128)S(1)} %select_maximum_fusion.2), kind=kLoop, calls=%fused_computation.4.clone.1 | loop fusion | flops 6289408 | bytes 8404992 | tf_op jit(solution)/shard_map/while/body/eval_jaxpr/reduce_sum | solution.py:94
  190.4 0.8 copy-done.1
  191.2 2.8 %fusion.52 = f32[8,256,64]{1,2,0:T(8,128)S(1)} fusion(f32[8,1024,256]{2,1,0:T(8,128)S(1)} %copy-done.1, f32[8,256]{1,0:T(8,128)S(1)} %select_maximum_fusion.2, bf16[4,1024,8,64]{1,3,2,0:T(8,128)(2,1)} %get-tuple-element.221, s32[]{:T(128)} %get-tuple-element.206, f32[8,256,64]{1,2,0:T(8,128)S(1)} %get-tuple-element.209, ...), kind=kOutput, calls=%fused_computation.8.clone.1 | convolution fusion | flops 275120128 | bytes 10502657 | tf_op jit(solution)/shard_map/while/body/eval_jaxpr/hpr,rhd->hpd/dot_general | solution.py:95
  194.0 5.8 %bitcast_reduce_fusion.2 = (f32[8,256]{1,0:T(8,128)S(1)}, f32[8,1024,256]{2,1,0:T(8,128)}) fusion(bf16[256,8,64]{0,2,1:T(8,128)(2,1)S(1)} %get-tuple-element.220, bf16[4,1024,8,64]{1,3,2,0:T(8,128)(2,1)} %get-tuple-element.219, s32[]{:T(128)} %get-tuple-element.206), kind=kOutput, calls=%fused_computation.1.clone.1 | convolution fusion | flops 272627712 | bytes 9708032 | tf_op jit(solution)/shard_map/while/body/eval_jaxpr/phd,rhd->hpr/dot_general | solution.py:88
  199.8 4.9 %fusion.50 = f32[8,256]{1,0:T(8,128)S(1)} fusion(f32[8,1024,256]{2,1,0:T(8,128)} %get-tuple-element.194, f32[8,256]{1,0:T(8,128)S(1)} %select_maximum_fusion.2), kind=kLoop, calls=%fused_computation.4.clone.1 | loop fusion | flops 6289408 | bytes 8404992 | tf_op jit(solution)/shard_map/while/body/eval_jaxpr/reduce_sum | solution.py:94
  204.8 0.8 copy-done.1
  205.6 2.8 %fusion.52 = f32[8,256,64]{1,2,0:T(8,128)S(1)} fusion(f32[8,1024,256]{2,1,0:T(8,128)S(1)} %copy-done.1, f32[8,256]{1,0:T(8,128)S(1)} %select_maximum_fusion.2, bf16[4,1024,8,64]{1,3,2,0:T(8,128)(2,1)} %get-tuple-element.221, s32[]{:T(128)} %get-tuple-element.206, f32[8,256,64]{1,2,0:T(8,128)S(1)} %get-tuple-element.209, ...), kind=kOutput, calls=%fused_computation.8.clone.1 | convolution fusion | flops 275120128 | bytes 10502657 | tf_op jit(solution)/shard_map/while/body/eval_jaxpr/hpr,rhd->hpd/dot_general | solution.py:95
  208.5 5.8 %bitcast_reduce_fusion.2 = (f32[8,256]{1,0:T(8,128)S(1)}, f32[8,1024,256]{2,1,0:T(8,128)}) fusion(bf16[256,8,64]{0,2,1:T(8,128)(2,1)S(1)} %get-tuple-element.220, bf16[4,1024,8,64]{1,3,2,0:T(8,128)(2,1)} %get-tuple-element.219, s32[]{:T(128)} %get-tuple-element.206), kind=kOutput, calls=%fused_computation.1.clone.1 | convolution fusion | flops 272627712 | bytes 9708032 | tf_op jit(solution)/shard_map/while/body/eval_jaxpr/phd,rhd->hpr/dot_general | solution.py:88
  214.2 4.9 %fusion.50 = f32[8,256]{1,0:T(8,128)S(1)} fusion(f32[8,1024,256]{2,1,0:T(8,128)} %get-tuple-element.194, f32[8,256]{1,0:T(8,128)S(1)} %select_maximum_fusion.2), kind=kLoop, calls=%fused_computation.4.clone.1 | loop fusion | flops 6289408 | bytes 8404992 | tf_op jit(solution)/shard_map/while/body/eval_jaxpr/reduce_sum | solution.py:94
  219.2 0.8 copy-done.1
  220.0 2.8 %fusion.52 = f32[8,256,64]{1,2,0:T(8,128)S(1)} fusion(f32[8,1024,256]{2,1,0:T(8,128)S(1)} %copy-done.1, f32[8,256]{1,0:T(8,128)S(1)} %select_maximum_fusion.2, bf16[4,1024,8,64]{1,3,2,0:T(8,128)(2,1)} %get-tuple-element.221, s32[]{:T(128)} %get-tuple-element.206, f32[8,256,64]{1,2,0:T(8,128)S(1)} %get-tuple-element.209, ...), kind=kOutput, calls=%fused_computation.8.clone.1 | convolution fusion | flops 275120128 | bytes 10502657 | tf_op jit(solution)/shard_map/while/body/eval_jaxpr/hpr,rhd->hpd/dot_general | solution.py:95
  222.8 0.1 divide_convert_fusion
  222.9 2.5 convolution_convert_fusion.1
  225.4 0.0 reduce-scatter.2.cloned.1.call-update
  225.4 0.0 copy-done.5
  225.4 0.1 dynamic_slice.29
  225.5 0.0 copy-done.4
  225.5 13.5 %reduce-scatter.2.cloned.1.call-done = bf16[256,512]{1,0:T(8,128)(2,1)} async-done(((bf16[256,1024]{1,0:T(8,128)(2,1)}), bf16[256,512]{1,0:T(8,128)(2,1)}) %reduce-scatter.2.cloned.1.call-update) | async-done | bytes 262160 | tf_op jit(solution)/shard_map/reduce_scatter | solution.py:129
  239.0 1.3 multiply_reduce_fusion.3
  240.3 3.8 %psum.7 = f32[256]{0:T(256)S(1)} all-reduce(f32[256]{0:T(256)S(1)} %multiply_reduce_fusion.3), channel_id=1, replica_groups=mesh['space'=16,'chan'=2] {'chan'}, use_global_device_ids=true, to_apply=%region_11.12 | all-reduce | flops 256 | bytes 2048 | tf_op jit(solution)/shard_map/psum | solution.py:133
  244.1 1.2 multiply_convert_fusion.2
  245.3 6.5 %all_gather.26 = bf16[256,1024]{1,0:T(8,128)(2,1)S(1)} all-gather(bf16[256,512]{1,0:T(8,128)(2,1)S(1)} %multiply_convert_fusion.2), channel_id=1, replica_groups=mesh['space'=16,'chan'=2] {'chan'}, dimensions={1}, use_global_device_ids=true | all-gather | bytes 786432 | tf_op jit(solution)/shard_map/all_gather | solution.py:138
  251.8 0.1 convert_element_type.178
  251.9 0.0 copy-done
  252.0 0.0 copy-done.6
  252.0 6.1 %fusion.23 = bf16[8,256,1024]{2,1,0:T(8,128)(2,1)} fusion(f32[8,1024]{1,0:T(8,128)S(1)} %copy-done.6, f32[8,1024]{1,0:T(8,128)S(1)} %broadcast_add_fusion, f32[256,1024]{1,0:T(8,128)S(1)} %convert_element_type.178, bf16[1024,1024]{1,0:T(8,128)(2,1)S(1)} %copy-done), kind=kOutput, calls=%fused_computation.30 | convolution fusion | flops 4303355904 | bytes 7405568 | tf_op jit(solution)/shard_map/dot_general | solution.py:142
  (31 shorter events, 0.2 us)
Async XLA Ops:
  6.5 245.4 %copy-start = (bf16[1024,1024]{1,0:T(8,128)(2,1)S(1)}, bf16[1024,1024]{1,0:T(8,128)(2,1)}, u32[]{:S(2)}) copy-start(bf16[1024,1024]{1,0:T(8,128)(2,1)} %param.21) | copy-start | bytes 6291460
  6.5 29.8 %copy-start.3 = (bf16[256,1024]{1,0:T(8,128)(2,1)S(1)}, bf16[256,1024]{1,0:T(8,128)(2,1)}, u32[]{:S(2)}) copy-start(bf16[256,1024]{1,0:T(8,128)(2,1)} %param.16) | copy-start | bytes 1572868
  6.5 32.5 %copy-start.7 = (f32[1024]{0:T(1024)S(1)}, f32[1024]{0:T(1024)}, u32[]{:S(2)}) copy-start(f32[1024]{0:T(1024)} %param.17) | copy-start | bytes 12292
  6.5 29.8 %all-gather.13.cloned.1.call-start = ((), (), s32[]{:S(2)}) async-start(), calls=%async_computation.4 | async-start | bytes 1572864 | tf_op jit(solution)/shard_map/all_gather | solution.py:17
  14.0 79.2 %all-gather.9.cloned.1.call-start = ((), (), s32[]{:S(2)}) async-start(), calls=%async_computation.1 | async-start | bytes 4456448 | tf_op jit(solution)/shard_map/all_gather | solution.py:108
  38.1 1.0 copy-start.2
  42.9 101.4 %all-gather.11.cloned.1.call-start = ((), (), s32[]{:S(2)}) async-start(), calls=%async_computation.2 | async-start | bytes 4456448 | tf_op jit(solution)/shard_map/all_gather | solution.py:109
  43.6 195.4 %reduce-scatter.2.cloned.1.call-start = ((), (), s32[]{:S(2)}) async-start(), calls=%async_computation.3 | async-start | bytes 786432 | tf_op jit(solution)/shard_map/reduce_scatter | solution.py:129
  165.2 60.2 %copy-start.5 = (f32[1024]{0:T(1024)S(1)}, f32[1024]{0:T(1024)}, u32[]{:S(2)}) copy-start(f32[1024]{0:T(1024)} %param.18) | copy-start | bytes 12292
  165.2 60.3 %copy-start.4 = (f32[8,1024]{1,0:T(8,128)S(1)}, f32[8,1024]{1,0:T(8,128)}, u32[]{:S(2)}) copy-start(f32[8,1024]{1,0:T(8,128)} %param.22) | copy-start | bytes 98308
  165.2 86.7 %copy-start.6 = (f32[8,1024]{1,0:T(8,128)S(1)}, f32[8,1024]{1,0:T(8,128)}, u32[]{:S(2)}) copy-start(f32[8,1024]{1,0:T(8,128)} %param.23) | copy-start | bytes 98308
  171.0 5.8 %copy-start.1 = (f32[8,1024,256]{2,1,0:T(8,128)S(1)}, f32[8,1024,256]{2,1,0:T(8,128)}, u32[]{:S(2)}) copy-start(f32[8,1024,256]{2,1,0:T(8,128)} %get-tuple-element.194) | copy-start | bytes 25165828 | tf_op jit(solution)/shard_map/while
  185.4 5.8 %copy-start.1 = (f32[8,1024,256]{2,1,0:T(8,128)S(1)}, f32[8,1024,256]{2,1,0:T(8,128)}, u32[]{:S(2)}) copy-start(f32[8,1024,256]{2,1,0:T(8,128)} %get-tuple-element.194) | copy-start | bytes 25165828 | tf_op jit(solution)/shard_map/while
  199.8 5.8 %copy-start.1 = (f32[8,1024,256]{2,1,0:T(8,128)S(1)}, f32[8,1024,256]{2,1,0:T(8,128)}, u32[]{:S(2)}) copy-start(f32[8,1024,256]{2,1,0:T(8,128)} %get-tuple-element.194) | copy-start | bytes 25165828 | tf_op jit(solution)/shard_map/while
  214.2 5.8 %copy-start.1 = (f32[8,1024,256]{2,1,0:T(8,128)S(1)}, f32[8,1024,256]{2,1,0:T(8,128)}, u32[]{:S(2)}) copy-start(f32[8,1024,256]{2,1,0:T(8,128)} %get-tuple-element.194) | copy-start | bytes 25165828 | tf_op jit(solution)/shard_map/while
Sparse Core Ops, SparseCore 0:
  14.1 22.2 all-gather.12
  43.0 50.0 all-gather.8
  95.3 48.9 all-gather.10
  225.5 13.4 reduce-scatter.1
where the time goes:
time: 270 us; the launch traced here: 265 us
  waiting for transfers between devices  105 us (39%)
  local copies, waits for them, and re-layouts  51.8 us (19%)
  matrix products  45.9 us (17%)
  other arithmetic  31.6 us (12%)
  blocking collectives  16.4 us (6%)
  between operations  13.3 us (5%)
    all_gather x1, waiting for transfers between devices, body(): key_piece = lax.all_gather(keys_mine, 'space', axis=0, tiled=True)  49.1 us
    all_gather x1, waiting for transfers between devices, body(): value_piece = lax.all_gather(values_mine, 'space', axis=0, tiled=True)  30.2 us
    unnamed x19, local copies, waits for them, and re-layouts  25.2 us
    dot_general x4, matrix products, attend_block(): jnp.einsum('phd,rhd->hpr', queries, key_block, preferred_element_type=jnp...  23 us
    reduce_sum x4, other arithmetic, attend_block(): run_sum = run_sum * rescale + jnp.sum(weights, -1)  19.7 us
    reduce_scatter x1, waiting for transfers between devices, body(): lax.psum_scatter(partial_out.astype(jnp.bfloat16), 'chan', scatter_dimens...  13.5 us
    all_gather x1, waiting for transfers between devices, merged(): lax.all_gather(part.astype(kind), axis)  11.5 us
    dot_general x4, matrix products, attend_block(): jnp.einsum('hpr,rhd->hpd', weights.astype(jnp.bfloat16), value_block, pre...  11.4 us
  transfers between devices with their start and end apart: 4, of which 4 were waited for; matrix products, arithmetic and copies ran while one was open for 10% of the time, Pallas kernels for 0%

commit v1 on v0

--- a/solution.py
+++ b/solution.py
@@ -1,8 +1,11 @@
+import functools
 import math
 
 import jax
 import jax.numpy as jnp
 from jax import lax
+from jax.experimental import pallas as pl
+from jax.experimental.pallas import tpu as pltpu
 from jax.sharding import PartitionSpec as P
 
 D = 1024
@@ -44,7 +47,7 @@
     )
 
 
-def body(
+def body_gather(
     patches,
     var_embed,
     agg_query,
@@ -145,6 +148,289 @@
     return decoded.reshape(var_count, pos_rows, d_model).astype(jnp.bfloat16)
 
 
+MESH = pl.DeviceIdType.MESH
+
+
+def attention_kernel(
+    chans, heads, qkv_ref, w_ref, mixed_ref, w_more_ref,
+    got, part, k_rows, v_cols, score_a, score_b, stage,
+    own_sem, send_sem, recv_sem, fwd_send, fwd_recv, out_send, out_recv,
+    w_send, w_recv, w_fsend, w_frecv,
+):
+    space = lax.axis_index("space")
+    chan = lax.axis_index("chan")
+    chip = space // 2
+    core = space % 2
+    partner = chip * 2 + (1 - core)
+    rows = qkv_ref.shape[3]
+    head_dim = qkv_ref.shape[2]
+    half = w_ref.shape[0] // 2
+
+    def same_core(step):
+        return lax.rem(chip + step, heads)
+
+    barrier = pltpu.get_barrier_semaphore()
+    count = 0
+    for step in range(heads):
+        for turn in range(chans):
+            if step == 0 and turn == 0:
+                continue
+            pl.semaphore_signal(
+                barrier, inc=1,
+                device_id={"space": same_core(step) * 2 + core, "chan": lax.rem(chan + turn, chans)},
+                device_id_type=MESH,
+            )
+            count += 1
+    pl.semaphore_signal(barrier, inc=1, device_id={"space": partner}, device_id_type=MESH)
+    pl.semaphore_wait(barrier, count + 1)
+
+    def block_out(step):
+        to = same_core(step)
+        return pltpu.make_async_remote_copy(
+            src_ref=qkv_ref.at[:, to], dst_ref=got.at[chip],
+            send_sem=send_sem.at[step], recv_sem=recv_sem.at[chip],
+            device_id={"space": to * 2 + core}, device_id_type=MESH,
+        )
+
+    def block_in(origin):
+        return pltpu.make_async_remote_copy(
+            src_ref=qkv_ref.at[:, chip], dst_ref=got.at[origin],
+            send_sem=send_sem.at[0], recv_sem=recv_sem.at[origin],
+            device_id={"space": partner}, device_id_type=MESH,
+        )
+
+    def forward(origin):
+        return pltpu.make_async_remote_copy(
+            src_ref=got.at[origin, pl.ds(1, 2)], dst_ref=part.at[origin],
+            send_sem=fwd_send.at[origin], recv_sem=fwd_recv.at[origin],
+            device_id={"space": partner}, device_id_type=MESH,
+        )
+
+    def w_out_copy(turn):
+        return pltpu.make_async_remote_copy(
+            src_ref=w_ref.at[pl.ds(core * half, half)],
+            dst_ref=w_more_ref.at[chans - turn - 1, pl.ds(core * half, half)],
+            send_sem=w_send.at[turn - 1], recv_sem=w_recv.at[chans - turn - 1],
+            device_id={"chan": lax.rem(chan + turn, chans)}, device_id_type=MESH,
+        )
+
+    def w_forward(slot, which):
+        return pltpu.make_async_remote_copy(
+            src_ref=w_more_ref.at[slot, pl.ds(which * half, half)],
+            dst_ref=w_more_ref.at[slot, pl.ds(which * half, half)],
+            send_sem=w_fsend.at[slot], recv_sem=w_frecv.at[slot],
+            device_id={"space": partner}, device_id_type=MESH,
+        )
+
+    own = pltpu.make_async_copy(qkv_ref.at[:, chip], got.at[chip], own_sem)
+    own.start()
+    for step in range(1, heads):
+        block_out(step).start()
+    for turn in range(1, chans):
+        w_out_copy(turn).start()
+    v_cols[:, pl.ds(head_dim, 16)] = jnp.ones_like(v_cols[:, pl.ds(head_dim, 16)])
+
+    def take(slot, keys, values):
+        k_rows[slot] = keys.T
+        v_cols[slot, pl.ds(0, head_dim)] = values
+
+    own.wait()
+    forward(chip).start()
+    take(chip, got[chip, 1], got[chip, 2])
+
+    @pl.loop(1, heads)
+    def _(step):
+        origin = lax.rem(chip + heads - step, heads)
+        block_in(origin).wait_recv()
+        forward(origin).start()
+        take(origin, got[origin, 1], got[origin, 2])
+
+    for slot in range(chans - 1):
+        w_out_copy(chans - 1 - slot).wait_recv()
+        w_forward(slot, core).start()
+
+    @pl.loop(0, heads)
+    def _(step):
+        origin = lax.rem(chip + heads - step, heads)
+        forward(origin).wait_recv()
+        take(heads + origin, part[origin, 0], part[origin, 1])
+
+    blocks = 2 * heads
+
+    def out_copy(step, turn):
+        return pltpu.make_async_remote_copy(
+            src_ref=stage.at[step], dst_ref=mixed_ref.at[(chans - turn) % chans, chip],
+            send_sem=out_send.at[step, turn], recv_sem=out_recv.at[(chans - turn) % chans, chip],
+            device_id={"space": same_core(step) * 2 + core, "chan": lax.rem(chan + turn, chans)},
+            device_id_type=MESH,
+        )
+
+    def out_wait(shift, origin):
+        return pltpu.make_async_remote_copy(
+            src_ref=stage.at[0], dst_ref=mixed_ref.at[shift, origin],
+            send_sem=out_send.at[0, 0], recv_sem=out_recv.at[shift, origin],
+            device_id={"space": partner}, device_id_type=MESH,
+        )
+
+    def first_pass(step, scores):
+        query = got[same_core(step), 0]
+
+        def one(t, top):
+            s = jnp.dot(k_rows[t], query, preferred_element_type=jnp.float32)
+            scores[t] = s
+            s_top = jnp.max(s.reshape(rows // 8, 8, rows), 0)
+            return s_top if top is None else jnp.maximum(top, s_top)
+
+        return one
+
+    def second_pass(scores, top):
+        def one(t, acc):
+            p = jnp.exp2(scores[t] - top).astype(jnp.bfloat16)
+            term = jnp.dot(v_cols[t], p, preferred_element_type=jnp.float32)
+            return term if acc is None else acc + term
+
+        return one
+
+    def both(step, scores_now, top_now, scores_next):
+        one_next = first_pass(step + 1, scores_next)
+        one_now = second_pass(scores_now, top_now)
+        top, acc = None, None
+        for t in range(blocks):
+            top = one_next(t, top)
+            acc = one_now(t, acc)
+        result = (acc[:head_dim] * (1.0 / acc[head_dim : head_dim + 1])).astype(jnp.bfloat16)
+        stage[step] = result
+
+        @pl.when(step == 0)
+        def _():
+            mixed_ref[0, chip] = result
+
+        @pl.when(step != 0)
+        def _():
+            out_copy(step, 0).start()
+
+        for turn in range(1, chans):
+            out_copy(step, turn).start()
+        return jnp.max(top, 0, keepdims=True)
+
+    one = first_pass(0, score_a)
+    top = None
+    for t in range(blocks):
+        top = one(t, top)
+    top = jnp.max(top, 0, keepdims=True)
+
+    def pair(i, top):
+        top = both(2 * i, score_a, top, score_b)
+        return both(2 * i + 1, score_b, top, score_a)
+
+    lax.fori_loop(0, heads // 2, pair, top)
+
+    for step in range(1, heads):
+        block_out(step).wait_send()
+        out_copy(step, 0).wait_send()
+        out_wait(0, same_core(step)).wait_recv()
+    for step in range(heads):
+        forward(step).wait_send()
+        for turn in range(1, chans):
+            out_copy(step, turn).wait_send()
+            out_wait(turn, step).wait_recv()
+    for slot in range(chans - 1):
+        w_out_copy(slot + 1).wait_send()
+        w_forward(slot, core).wait_send()
+        w_forward(slot, 1 - core).wait_recv()
+
+
+def attention(qkv, w_out, chans):
+    _, heads, head_dim, rows = qkv.shape
+    dma = pltpu.SemaphoreType.DMA
+    vmem = pl.BlockSpec(memory_space=pltpu.VMEM)
+    hbm = pl.BlockSpec(memory_space=pl.ANY)
+    bf16 = jnp.bfloat16
+    return pl.pallas_call(
+        functools.partial(attention_kernel, chans, heads),
+        out_shape=(
+            jax.ShapeDtypeStruct((chans, heads, head_dim, rows), bf16),
+            jax.ShapeDtypeStruct((chans - 1,) + w_out.shape, bf16),
+        ),
+        in_specs=[vmem, hbm],
+        out_specs=(vmem, hbm),
+        scratch_shapes=[
+            pltpu.VMEM((heads, 3, head_dim, rows), bf16),
+            pltpu.VMEM((heads, 2, head_dim, rows), bf16),
+            pltpu.VMEM((2 * heads, rows, head_dim), bf16),
+            pltpu.VMEM((2 * heads, head_dim + 16, rows), bf16),
+            pltpu.VMEM((2 * heads, rows, rows), jnp.float32),
+            pltpu.VMEM((2 * heads, rows, rows), jnp.float32),
+            pltpu.VMEM((heads, head_dim, rows), bf16),
+            dma, dma((heads,)), dma((heads,)), dma((heads,)), dma((heads,)),
+            dma((heads, chans)), dma((chans, heads)),
+            dma((chans - 1,)), dma((chans - 1,)), dma((chans - 1,)), dma((chans - 1,)),
+        ],
+        compiler_params=pltpu.CompilerParams(
+            collective_id=0, has_side_effects=True, vmem_limit_bytes=48 * 1024 * 1024
+        ),
+    )(qkv, w_out)
+
+
+def body_exchange(
+    patches,
+    var_embed,
+    agg_query,
+    pos_embed,
+    gain_first,
+    gain_second,
+    w_qkv,
+    w_out,
+    w_dec,
+    mod_scale,
+    mod_shift,
+):
+    var_count, pos_rows, d_model = patches.shape
+    chans = lax.axis_size("chan")
+    embedded = patches.astype(jnp.float32) + var_embed[:, None, :]
+    logits = jnp.sum(embedded * agg_query, -1) * (1.0 / math.sqrt(D))
+    local_top = jnp.max(logits, 0)
+    expo_terms = jnp.exp(logits - local_top)
+    part_sum = jnp.sum(expo_terms, 0)
+    part_acc = jnp.sum(expo_terms[:, :, None] * embedded, 0)
+    state = (local_top, part_sum, part_acc)
+    sent = part_acc.astype(jnp.bfloat16)
+    stats = jnp.stack([local_top, part_sum])
+    for turn in range(1, chans):
+        ring = [(i, (i + turn) % chans) for i in range(chans)]
+        there = lax.ppermute(sent, "chan", ring).astype(jnp.float32)
+        there_stats = lax.ppermute(stats, "chan", ring)
+        state = pool_combine(state, (there_stats[0], there_stats[1], there))
+    _, denom_sum, pooled_acc = state
+    resid = pooled_acc / denom_sum[:, None] + pos_embed.astype(jnp.float32)
+    normed = rms_norm(resid, gain_first).astype(jnp.bfloat16)
+    columns = w_qkv.shape[2]
+    head_dim = D // HEADS
+    head_count = columns // head_dim
+    factor = jnp.array([math.log2(math.e) / math.sqrt(head_dim), 1.0, 1.0], jnp.float32)
+    qkv = lax.dot_general(
+        w_qkv.reshape(d_model, 3 * columns), normed, (((0,), (1,)), ((), ())),
+        preferred_element_type=jnp.float32,
+    ).reshape(3, head_count, head_dim, pos_rows)
+    qkv = (qkv * factor[:, None, None, None]).astype(jnp.bfloat16)
+    mixed, w_more = attention(qkv, w_out, chans)
+    mixed = mixed.reshape(chans, columns, pos_rows)
+    trunk = resid
+    for shift in range(chans):
+        trunk = trunk + lax.dot_general(
+            mixed[shift], w_out if shift == 0 else w_more[shift - 1], (((0,), (0,)), ((), ())),
+            preferred_element_type=jnp.float32,
+        )
+    normed_two = rms_norm(trunk, gain_second).astype(jnp.bfloat16)
+    modulated = (
+        normed_two.astype(jnp.float32)[None] * (1.0 + mod_scale[:, None, :]) + mod_shift[:, None, :]
+    ).astype(jnp.bfloat16)
+    decoded = jnp.dot(
+        modulated.reshape(var_count * pos_rows, d_model), w_dec, preferred_element_type=jnp.float32
+    )
+    return decoded.reshape(var_count, pos_rows, d_model).astype(jnp.bfloat16)
+
+
 def solution(mesh):
     placed = (
         P("chan", "space", None),
@@ -159,6 +445,8 @@
         P("chan", None),
         P("chan", None),
     )
+    per_chan = HEADS // mesh.shape["chan"]
+    body = body_exchange if mesh.shape["space"] == 2 * per_chan else body_gather
     return jax.shard_map(
         body, mesh=mesh, in_specs=placed, out_specs=P("chan", "space", None), check_vma=False
     )

time: 270 us -> 80.2 us (0.30); the launches traced: 265 us -> 79.9 us
  waiting for transfers between devices: 105 us -> 7.94 us
  local copies, waits for them, and re-layouts: 51.8 us -> 8.79 us
  Pallas kernels: 0 us -> 41 us
  matrix products: 45.9 us -> 11.2 us
  other arithmetic: 31.6 us -> 9.29 us
  blocking collectives: 16.4 us -> 0 us
  between operations: 13.3 us -> 0.17 us
    all_gather x3 -> x0, waiting for transfers between devices: 90.8 us -> none  [the longest x1 49.1 us: body(): key_piece = lax.all_gather(keys_mine, 'space', axis=0, tiled=True)]
    pallas_call x0 -> x1, Pallas kernels: none -> 41 us  [attention(): pl.pallas_call(functools.partial(attention_kernel, chans, heads), out_sha...]
    dot_general x11 -> x4, matrix products: 45.9 us -> 11.2 us  [the longest x1 6.03 us: body_exchange(): jnp.dot(modulated.reshape(var_count * pos_rows, d_model), w_dec, preferre...]
    reduce_sum x8 -> x3, other arithmetic: 28.4 us -> 4.83 us  [the longest x1 3.51 us: body_exchange(): logits = jnp.sum(embedded * agg_query, -1) * (1.0 / math.sqrt(D))]
    another operation x2 -> x0, local copies, waits for them, and re-layouts: 22.4 us -> none  [the longest x1 11.2 us: body(): key_stack = key_heads.reshape(blocks, 1024, head_count, head_dim)]
    unnamed x19 -> x23, local copies, waits for them, and re-layouts: 25.2 us -> 5.63 us
    reduce_scatter x1 -> x0, waiting for transfers between devices: 13.5 us -> none  [body(): lax.psum_scatter(partial_out.astype(jnp.bfloat16), 'chan', scatter_dimens...]
    all_gather x3 -> x0, blocking collectives: 12.7 us -> none  [the longest x1 6.52 us: body(): normed_two = lax.all_gather(normed_part, 'chan', axis=1, tiled=True)]
  transfers between devices with their start and end apart: 4 -> 2, of which waited for: 4 -> 1; matrix products, arithmetic and copies ran while one was open for 10% -> 9% of each run, Pallas kernels for 0% -> 0%
where the time goes in v1:
time: 80.2 us; the launch traced here: 79.9 us
  Pallas kernels  41 us (51%)
  matrix products  11.2 us (14%)
  other arithmetic  9.29 us (12%)
  local copies, waits for them, and re-layouts  8.79 us (11%)
  waiting for transfers between devices  7.94 us (10%)
  starting transfers between devices  1.53 us (2%)
    pallas_call x1, Pallas kernels, attention(): pl.pallas_call(functools.partial(attention_kernel, chans, heads), out_sha...  41 us
    ppermute x1, waiting for transfers between devices, body_exchange(): there = lax.ppermute(sent, 'chan', ring).astype(jnp.float32)  7.94 us
    dot_general x1, matrix products, body_exchange(): jnp.dot(modulated.reshape(var_count * pos_rows, d_model), w_dec, preferre...  6.03 us
    unnamed x23, local copies, waits for them, and re-layouts  5.63 us
    dot_general x1, matrix products, body_exchange(): lax.dot_general(w_qkv.reshape(d_model, 3 * columns), normed, (((0,), (1,)...  4.13 us
    reduce_sum x1, other arithmetic, body_exchange(): logits = jnp.sum(embedded * agg_query, -1) * (1.0 / math.sqrt(D))  3.51 us
    dot_general x1, local copies, waits for them, and re-layouts, body_exchange(): lax.dot_general(w_qkv.reshape(d_model, 3 * columns), normed, (((0,), (1,)...  3.11 us
    convert_element_type x1, other arithmetic, body_exchange(): qkv = (qkv * factor[:, None, None, None]).astype(jnp.bfloat16)  1.71 us
  transfers between devices with their start and end apart: 2, of which 1 were waited for; matrix products, arithmetic and copies ran while one was open for 9% of the time, Pallas kernels for 0%

profile of v1, /device:TPU:11, one launch (start us, length us, event | category | flops | bytes accessed | tf_op | source)
XLA Modules:
  0.0 79.9 jit_solution(11043030998473275916)
XLA Ops:
  0.0 0.0 copy-start
  0.0 0.0 copy-start.2
  0.0 0.0 copy-start.5
  0.0 3.5 %multiply_reduce_fusion.1 = f32[8,256]{1,0:T(8,128)S(1)} fusion(bf16[8,256,1024]{2,1,0:T(8,128)(2,1)} %param.12, f32[1024]{0:T(1024)} %param.14, f32[8,1024]{1,0:T(8,128)} %param.13), kind=kLoop, calls=%fused_computation.2 | loop fusion | flops 8386560 | bytes 4239360 | tf_op jit(solution)/shard_map/reduce_sum | solution.py:391
  3.5 0.0 copy-start.6
  3.6 1.3 %collective-permute-start = (f32[2,256]{1,0:T(2,128)S(1)}, f32[2,256]{1,0:T(2,128)S(1)}, u32[]{:S(2)}, u32[]{:S(2)}) collective-permute-start(f32[2,256]{1,0:T(2,128)S(1)} %pad_maximum_fusion), channel_id=1, source_target_pairs={{0,1},{1,0},{2,3},{3,2},{4,5},{5,4},{6,7},{7,6},{8,9},{9,8},{10,11... | collective-permute-start | bytes 6152 | tf_op jit(solution)/shard_map/ppermute | solution.py:402
  4.9 0.0 copy-done.2
  4.9 0.0 copy-done.5
  4.9 1.3 %multiply_reduce_fusion = f32[256,1024]{1,0:T(8,128)S(1)} fusion(bf16[8,256,1024]{2,1,0:T(8,128)(2,1)S(1)} %copy-done.2, f32[8,256]{1,0:T(8,128)S(1)} %get-tuple-element.15, f32[8,1024]{1,0:T(8,128)S(1)} %copy-done.5), kind=kLoop, calls=%fused_computation.1 | loop fusion | flops 8126464 | bytes 5283840 | tf_op jit(solution)/shard_map/reduce_sum | solution.py:395
  6.2 0.9 %convert_element_type.33 = bf16[256,1024]{1,0:T(8,128)(2,1)} convert(f32[256,1024]{1,0:T(8,128)S(1)} %multiply_reduce_fusion) | non-fusion elementwise | flops 262144 | bytes 1572864 | tf_op jit(solution)/shard_map/convert_element_type | solution.py:397
  7.1 0.2 collective-permute-start.1
  7.3 0.0 copy-done.6
  7.3 0.0 copy-start.8
  7.3 4.6 %copy.14 = bf16[1024,3,512]{0,2,1:T(8,128)(2,1)} copy(bf16[1024,3,512]{2,0,1:T(8,128)(2,1)} %param.18) | data formatting | bytes 6291456 | tf_op args[6]
  12.0 0.0 collective-permute-done
  12.0 7.9 %collective-permute-done.1 = bf16[256,1024]{1,0:T(8,128)(2,1)} collective-permute-done((bf16[256,1024]{1,0:T(8,128)(2,1)}, bf16[256,1024]{1,0:T(8,128)(2,1)}, u32[]{:S(2)}, u32[]{:S(2)}) %collective-permute-start.1) | collective-permute-done | bytes 524320 | tf_op jit(solution)/shard_map/ppermute | solution.py:401
  19.9 1.7 %multiply_reduce_fusion.3 = (f32[256]{0:T(256)S(1)}, f32[256,1024]{1,0:T(8,128)S(1)}) fusion(bf16[256,1024]{1,0:T(8,128)(2,1)} %param.15, f32[256]{0:T(256)S(1)} %get-tuple-element.11, f32[256]{0:T(256)S(1)} %get-tuple-element.13, bf16[256,1024]{1,0:T(8,128)(2,1)} %collective-permute-done.1, f32[256,1024]{1,0:T(8,128)S(1)} %multiply_reduce_fusion, ...), kind=kLoop, calls=%fused_computation.18 | loop fusion | flops 2359040 | bytes 3149824 | tf_op jit(solution)/shard_map/reduce_sum | solution.py:34
  21.6 0.0 copy-start.3
  21.6 0.9 %copy-done.3 = f32[256,1024]{1,0:T(8,128)} copy-done((f32[256,1024]{1,0:T(8,128)}, f32[256,1024]{1,0:T(8,128)S(1)}, u32[]{:S(2)}) %copy-start.3) | copy-done | bytes 1048600
  22.6 0.0 copy-done.8
  22.6 0.0 copy-start.9
  22.6 4.1 %convolution_bitcast_fusion = f32[1536,256]{0,1:T(8,128)} fusion(bf16[1024,1536]{0,1:T(8,128)(2,1)} %bitcast.22, f32[256,1024]{1,0:T(8,128)S(1)} %get-tuple-element.10, f32[1024]{0:T(1024)S(1)} %copy-done.8, f32[256]{0:T(256)S(1)} %add_rsqrt_fusion.1), kind=kOutput, calls=%fused_computation.8 | convolution fusion | flops 806092800 | bytes 5772288 | tf_op jit(solution)/shard_map/dot_general | solution.py:411
  26.7 0.0 copy-start.1
  26.7 3.1 %copy.15 = f32[1536,256]{1,0:T(8,128)} copy(f32[1536,256]{0,1:T(8,128)} %convolution_bitcast_fusion) | data formatting | bytes 3145728 | tf_op jit(solution)/shard_map/dot_general | solution.py:411
  29.8 0.0 copy-start.4
  29.8 0.0 copy-done.9
  29.8 1.7 %multiply_convert_fusion.qkv_ref = bf16[3,8,64,256]{3,2,1,0:T(8,128)(2,1)S(1)} fusion(f32[3,8,64,256]{3,2,1,0:T(8,128)} %bitcast.23, f32[3]{0:T(128)S(1)} %copy-done.9), kind=kLoop, calls=%fused_computation.11 | loop fusion | flops 786432 | bytes 2359308 | tf_op jit(solution)/shard_map/convert_element_type | solution.py:415
  31.5 0.0 copy-done.1
  31.5 41.0 %shard_map.118 = (bf16[2,8,64,256]{3,2,1,0:T(8,128)(2,1)S(1)}, bf16[1,512,1024]{2,1,0:T(8,128)(2,1)S(1)}) custom-call(bf16[3,8,64,256]{3,2,1,0:T(8,128)(2,1)S(1)} %multiply_convert_fusion.qkv_ref, bf16[512,1024]{1,0:T(8,128)(2,1)S(1)} %copy-done.1), custom_call_target="tpu_custom_call" | custom-call | tf_op jit(solution)/shard_map/pallas_call | solution.py:349
  72.6 0.0 copy-start.7
  72.6 0.0 copy-done.4
  72.6 0.0 copy-start.10
  72.7 0.5 convolution_add_fusion.1
  73.1 0.6 multiply_reduce_fusion.2
  73.7 0.0 copy-done.7
  73.7 0.2 fusion.7
  73.9 0.0 copy-done
  73.9 0.0 copy-done.10
  73.9 6.0 %fusion.4 = bf16[8,256,1024]{2,1,0:T(8,128)(2,1)} fusion(f32[8,1024]{1,0:T(8,128)S(1)} %copy-done.10, f32[8,1024]{1,0:T(8,128)S(1)} %broadcast_add_fusion, f32[256,1024]{1,0:T(8,128)S(1)} %fusion.7, bf16[1024,1024]{1,0:T(8,128)(2,1)S(1)} %copy-done), kind=kOutput, calls=%fused_computation.9 | convolution fusion | flops 4303355904 | bytes 7405568 | tf_op jit(solution)/shard_map/dot_general | solution.py:428
  (9 shorter events, 0.1 us)
Async XLA Ops:
  0.0 73.9 %copy-start = (bf16[1024,1024]{1,0:T(8,128)(2,1)S(1)}, bf16[1024,1024]{1,0:T(8,128)(2,1)}, u32[]{:S(2)}) copy-start(bf16[1024,1024]{1,0:T(8,128)(2,1)} %param.20) | copy-start | bytes 6291460
  0.0 4.9 %copy-start.2 = (bf16[8,256,1024]{2,1,0:T(8,128)(2,1)S(1)}, bf16[8,256,1024]{2,1,0:T(8,128)(2,1)}, u32[]{:S(2)}) copy-start(bf16[8,256,1024]{2,1,0:T(8,128)(2,1)} %param.12) | copy-start | bytes 12582916
  0.0 4.9 %copy-start.5 = (f32[8,1024]{1,0:T(8,128)S(1)}, f32[8,1024]{1,0:T(8,128)}, u32[]{:S(2)}) copy-start(f32[8,1024]{1,0:T(8,128)} %param.13) | copy-start | bytes 98308
  3.5 3.8 %copy-start.6 = (f32[8,1024]{1,0:T(8,128)S(1)}, f32[8,1024]{1,0:T(8,128)}, u32[]{:S(2)}) copy-start(f32[8,1024]{1,0:T(8,128)} %param.21) | copy-start | bytes 98308
  3.6 8.4 %collective-permute-start = (f32[2,256]{1,0:T(2,128)S(1)}, f32[2,256]{1,0:T(2,128)S(1)}, u32[]{:S(2)}, u32[]{:S(2)}) collective-permute-start(f32[2,256]{1,0:T(2,128)S(1)} %pad_maximum_fusion), channel_id=1, source_target_pairs={{0,1},{1,0},{2,3},{3,2},{4,5},{5,4},{6,7},{7,6},{8,9},{9,8},{10,11... | collective-permute-start | bytes 6152 | tf_op jit(solution)/shard_map/ppermute | solution.py:402
  7.1 12.8 %collective-permute-start.1 = (bf16[256,1024]{1,0:T(8,128)(2,1)}, bf16[256,1024]{1,0:T(8,128)(2,1)}, u32[]{:S(2)}, u32[]{:S(2)}) collective-permute-start(bf16[256,1024]{1,0:T(8,128)(2,1)} %convert_element_type.33), channel_id=1, source_target_pairs={{0,1},{1,0},{2,3},{3,2},{4,5},{5,4},{6,7},{7,6},{8,9},{9,8},{10,11... | collective-permute-start | bytes 1572872 | tf_op jit(solution)/shard_map/ppermute | solution.py:401
  7.3 15.2 %copy-start.8 = (f32[1024]{0:T(1024)S(1)}, f32[1024]{0:T(1024)}, u32[]{:S(2)}) copy-start(f32[1024]{0:T(1024)} %param.16) | copy-start | bytes 12292
  21.6 1.0 %copy-start.3 = (f32[256,1024]{1,0:T(8,128)}, f32[256,1024]{1,0:T(8,128)S(1)}, u32[]{:S(2)}) copy-start(f32[256,1024]{1,0:T(8,128)S(1)} %get-tuple-element.10) | copy-start | bytes 3145732
  22.6 7.2 %copy-start.9 = (f32[3]{0:T(128)S(1)}, f32[3]{0:T(128)}, u32[]{:S(2)}) copy-start(f32[3]{0:T(128)} %constant.16.clone) | copy-start | bytes 40
  26.7 4.8 %copy-start.1 = (bf16[512,1024]{1,0:T(8,128)(2,1)S(1)}, bf16[512,1024]{1,0:T(8,128)(2,1)}, u32[]{:S(2)}) copy-start(bf16[512,1024]{1,0:T(8,128)(2,1)} %w_ref.1) | copy-start | bytes 3145732
  29.8 42.8 %copy-start.4 = (f32[256,1024]{1,0:T(8,128)S(1)}, f32[256,1024]{1,0:T(8,128)}, u32[]{:S(2)}) copy-start(f32[256,1024]{1,0:T(8,128)} %copy-done.3) | copy-start | bytes 3145732
  72.6 1.1 %copy-start.7 = (f32[1024]{0:T(1024)S(1)}, f32[1024]{0:T(1024)}, u32[]{:S(2)}) copy-start(f32[1024]{0:T(1024)} %param.17) | copy-start | bytes 12292
  72.6 1.2 %copy-start.10 = (f32[8,1024]{1,0:T(8,128)S(1)}, f32[8,1024]{1,0:T(8,128)}, u32[]{:S(2)}) copy-start(f32[8,1024]{1,0:T(8,128)} %param.22) | copy-start | bytes 98308

commit v2 on v1

--- a/solution.py
+++ b/solution.py
@@ -149,12 +149,17 @@
 
 
 MESH = pl.DeviceIdType.MESH
-
-
-def attention_kernel(
-    chans, heads, qkv_ref, w_ref, mixed_ref, w_more_ref,
+PARTS = 4
+
+
+def fused_kernel(
+    chans, heads,
+    patches_ref, embed_ref, query_ref, pos_ref, gain_ref, w_qkv_ref, w_ref,
+    mixed_ref, w_more_ref, resid_ref,
+    tokens, w_qkv, pos, acc, acc_out, acc_in, stat, stat_in, acc_stat, normed, qkv_ref,
     got, part, k_rows, v_cols, score_a, score_b, stage,
-    own_sem, send_sem, recv_sem, fwd_send, fwd_recv, out_send, out_recv,
+    load_sem, acc_send, acc_recv, stat_send, stat_recv,
+    send_sem, recv_sem, fwd_send, fwd_recv, out_send, out_recv,
     w_send, w_recv, w_fsend, w_frecv,
 ):
     space = lax.axis_index("space")
@@ -162,12 +167,27 @@
     chip = space // 2
     core = space % 2
     partner = chip * 2 + (1 - core)
-    rows = qkv_ref.shape[3]
+    var_count, rows, d_model = tokens.shape
     head_dim = qkv_ref.shape[2]
+    columns = heads * head_dim
     half = w_ref.shape[0] // 2
+    part_rows = rows // PARTS
+    half_rows = rows // 2
 
     def same_core(step):
         return lax.rem(chip + step, heads)
+
+    loads = [
+        pltpu.make_async_copy(
+            patches_ref.at[:, pl.ds(c * part_rows, part_rows)],
+            tokens.at[:, pl.ds(c * part_rows, part_rows)], load_sem.at[c],
+        )
+        for c in range(PARTS)
+    ]
+    load_w = pltpu.make_async_copy(w_qkv_ref, w_qkv, load_sem.at[PARTS])
+    load_pos = pltpu.make_async_copy(pos_ref, pos, load_sem.at[PARTS + 1])
+    for copy in loads + [load_pos, load_w]:
+        copy.start()
 
     barrier = pltpu.get_barrier_semaphore()
     count = 0
@@ -182,27 +202,45 @@
             )
             count += 1
     pl.semaphore_signal(barrier, inc=1, device_id={"space": partner}, device_id_type=MESH)
-    pl.semaphore_wait(barrier, count + 1)
-
-    def block_out(step):
+
+    def acc_copy(c, turn):
+        place = pl.ds(c * part_rows, part_rows)
+        return pltpu.make_async_remote_copy(
+            src_ref=acc_out.at[place], dst_ref=acc_in.at[chans - turn - 1, place],
+            send_sem=acc_send.at[c, turn - 1], recv_sem=acc_recv.at[c, chans - turn - 1],
+            device_id={"chan": lax.rem(chan + turn, chans)}, device_id_type=MESH,
+        )
+
+    def stat_copy(h, turn):
+        return pltpu.make_async_remote_copy(
+            src_ref=stat.at[h, pl.ds(0, 8)], dst_ref=stat_in.at[h, chans - turn - 1],
+            send_sem=stat_send.at[h, turn - 1], recv_sem=stat_recv.at[h, chans - turn - 1],
+            device_id={"chan": lax.rem(chan + turn, chans)}, device_id_type=MESH,
+        )
+
+    def lanes_of(h):
+        return pl.ds(h * half_rows, half_rows)
+
+    def block_out(h, step):
         to = same_core(step)
         return pltpu.make_async_remote_copy(
-            src_ref=qkv_ref.at[:, to], dst_ref=got.at[chip],
-            send_sem=send_sem.at[step], recv_sem=recv_sem.at[chip],
+            src_ref=qkv_ref.at[:, to, :, lanes_of(h)], dst_ref=got.at[chip, :, :, lanes_of(h)],
+            send_sem=send_sem.at[h, step], recv_sem=recv_sem.at[h, chip],
             device_id={"space": to * 2 + core}, device_id_type=MESH,
         )
 
-    def block_in(origin):
-        return pltpu.make_async_remote_copy(
-            src_ref=qkv_ref.at[:, chip], dst_ref=got.at[origin],
-            send_sem=send_sem.at[0], recv_sem=recv_sem.at[origin],
+    def block_in(h, origin):
+        return pltpu.make_async_remote_copy(
+            src_ref=qkv_ref.at[:, chip, :, lanes_of(h)], dst_ref=got.at[origin, :, :, lanes_of(h)],
+            send_sem=send_sem.at[h, 0], recv_sem=recv_sem.at[h, origin],
             device_id={"space": partner}, device_id_type=MESH,
         )
 
-    def forward(origin):
-        return pltpu.make_async_remote_copy(
-            src_ref=got.at[origin, pl.ds(1, 2)], dst_ref=part.at[origin],
-            send_sem=fwd_send.at[origin], recv_sem=fwd_recv.at[origin],
+    def forward(h, origin):
+        return pltpu.make_async_remote_copy(
+            src_ref=got.at[origin, pl.ds(1, 2), :, lanes_of(h)],
+            dst_ref=part.at[origin, :, :, lanes_of(h)],
+            send_sem=fwd_send.at[h, origin], recv_sem=fwd_recv.at[h, origin],
             device_id={"space": partner}, device_id_type=MESH,
         )
 
@@ -222,38 +260,120 @@
             device_id={"space": partner}, device_id_type=MESH,
         )
 
-    own = pltpu.make_async_copy(qkv_ref.at[:, chip], got.at[chip], own_sem)
-    own.start()
-    for step in range(1, heads):
-        block_out(step).start()
+    v_cols[:, pl.ds(head_dim, 16)] = jnp.ones_like(v_cols[:, pl.ds(head_dim, 16)])
+    group = 16
+    lane = lax.broadcasted_iota(jnp.int32, (group, 128), 1)
+    agg_query = query_ref[...]
+
+    def pool(c):
+        @pl.loop(0, part_rows // group)
+        def _(i):
+            at = pl.ds(pl.multiple_of(c * part_rows + i * group, group), group)
+            logits = []
+            for v in range(var_count):
+                embedded = tokens[v, at].astype(jnp.float32) + embed_ref[pl.ds(v, 1)]
+                logits.append(
+                    jnp.sum(embedded * agg_query, -1, keepdims=True) * (1.0 / math.sqrt(D))
+                )
+            top = functools.reduce(jnp.maximum, logits)
+            total, weighted = None, None
+            for v in range(var_count):
+                embedded = tokens[v, at].astype(jnp.float32) + embed_ref[pl.ds(v, 1)]
+                weight = jnp.exp(logits[v] - top)
+                total = weight if v == 0 else total + weight
+                weighted = weight * embedded if v == 0 else weighted + weight * embedded
+            acc[at] = weighted
+            acc_out[at] = weighted.astype(jnp.bfloat16)
+            resid_ref[at, pl.ds(0, 128)] = jnp.where(lane == 0, top, total)
+
+    for c in range(PARTS):
+        loads[c].wait()
+        pool(c)
+        if c == 0:
+            pl.semaphore_wait(barrier, count + 1)
+        for turn in range(1, chans):
+            acc_copy(c, turn).start()
+        if c % (PARTS // 2) == PARTS // 2 - 1:
+            h = c // (PARTS // 2)
+            stat[h] = resid_ref[lanes_of(h), pl.ds(0, 128)].T
+            for turn in range(1, chans):
+                stat_copy(h, turn).start()
+
+    def take(slot, h, keys, values):
+        k_rows[slot, lanes_of(h)] = keys.T
+        v_cols[slot, pl.ds(0, head_dim), lanes_of(h)] = values
+
+    load_pos.wait()
+    gain = gain_ref[...]
+    spread = 128
+    for h in range(2):
+        for slot in range(chans - 1):
+            stat_copy(h, chans - 1 - slot).wait_recv()
+            for c in range(h * PARTS // 2, (h + 1) * PARTS // 2):
+                acc_copy(c, chans - 1 - slot).wait_recv()
+
+        for slot in range(chans - 1):
+            stat_ref = stat_in.at[h, slot]
+            wide = jnp.concatenate([stat_ref[...]] * (spread // 8), 0).T
+            acc_stat[slot] = wide
+
+        @pl.loop(0, half_rows // group)
+        def _(i):
+            near = pl.ds(pl.multiple_of(i * group, group), group)
+            at = pl.ds(pl.multiple_of(h * half_rows + i * group, group), group)
+            own = resid_ref[at, pl.ds(0, 128)]
+            tops, totals = [own[:, 0:1]], [own[:, 1:2]]
+            for slot in range(chans - 1):
+                other = acc_stat[slot, near]
+                tops.append(other[:, 0:1])
+                totals.append(other[:, 1:2])
+            top = functools.reduce(jnp.maximum, tops)
+            factors = [jnp.exp(t - top) for t in tops]
+            denom = functools.reduce(jnp.add, [f * t for f, t in zip(factors, totals)])
+            pooled = acc[at] * (factors[0] / denom)
+            for slot in range(chans - 1):
+                pooled += acc_in[slot, at].astype(jnp.float32) * (factors[slot + 1] / denom)
+            resid = pooled + pos[at].astype(jnp.float32)
+            resid_ref[at] = resid
+            normed[near] = rms_norm(resid, gain).astype(jnp.bfloat16)
+
+        if h == 0:
+            load_w.wait()
+        for j in range(3):
+            out = jnp.dot(
+                normed[...], w_qkv[:, pl.ds(j * columns, columns)],
+                preferred_element_type=jnp.float32,
+            )
+            if j == 0:
+                out = out * (math.log2(math.e) / math.sqrt(head_dim))
+            qkv_ref[j, :, :, lanes_of(h)] = (
+                out.T.astype(jnp.bfloat16).reshape(heads, head_dim, half_rows)
+            )
+        for step in range(1, heads):
+            block_out(h, step).start()
+        got[chip, :, :, lanes_of(h)] = qkv_ref[:, chip, :, lanes_of(h)]
+        forward(h, chip).start()
+        take(chip, h, got[chip, 1, :, lanes_of(h)], got[chip, 2, :, lanes_of(h)])
+
     for turn in range(1, chans):
         w_out_copy(turn).start()
-    v_cols[:, pl.ds(head_dim, 16)] = jnp.ones_like(v_cols[:, pl.ds(head_dim, 16)])
-
-    def take(slot, keys, values):
-        k_rows[slot] = keys.T
-        v_cols[slot, pl.ds(0, head_dim)] = values
-
-    own.wait()
-    forward(chip).start()
-    take(chip, got[chip, 1], got[chip, 2])
-
-    @pl.loop(1, heads)
-    def _(step):
-        origin = lax.rem(chip + heads - step, heads)
-        block_in(origin).wait_recv()
-        forward(origin).start()
-        take(origin, got[origin, 1], got[origin, 2])
-
-    for slot in range(chans - 1):
-        w_out_copy(chans - 1 - slot).wait_recv()
-        w_forward(slot, core).start()
-
-    @pl.loop(0, heads)
-    def _(step):
-        origin = lax.rem(chip + heads - step, heads)
-        forward(origin).wait_recv()
-        take(heads + origin, part[origin, 0], part[origin, 1])
+
+    for h in range(2):
+        @pl.loop(1, heads)
+        def _(step):
+            origin = lax.rem(chip + heads - step, heads)
+            block_in(h, origin).wait_recv()
+            forward(h, origin).start()
+            take(origin, h, got[origin, 1, :, lanes_of(h)], got[origin, 2, :, lanes_of(h)])
+
+    for h in range(2):
+        @pl.loop(0, heads)
+        def _(step):
+            origin = lax.rem(chip + heads - step, heads)
+            forward(h, origin).wait_recv()
+            take(
+                heads + origin, h, part[origin, 0, :, lanes_of(h)], part[origin, 1, :, lanes_of(h)]
+            )
 
     blocks = 2 * heads
 
@@ -323,14 +443,20 @@
         top = both(2 * i, score_a, top, score_b)
         return both(2 * i + 1, score_b, top, score_a)
 
-    lax.fori_loop(0, heads // 2, pair, top)
+    top = lax.fori_loop(0, heads // 4, pair, top)
+    for slot in range(chans - 1):
+        w_out_copy(chans - 1 - slot).wait_recv()
+        w_forward(slot, core).start()
+    lax.fori_loop(heads // 4, heads // 2, pair, top)
 
     for step in range(1, heads):
-        block_out(step).wait_send()
+        for h in range(2):
+            block_out(h, step).wait_send()
         out_copy(step, 0).wait_send()
         out_wait(0, same_core(step)).wait_recv()
     for step in range(heads):
-        forward(step).wait_send()
+        for h in range(2):
+            forward(h, step).wait_send()
         for turn in range(1, chans):
             out_copy(step, turn).wait_send()
             out_wait(turn, step).wait_recv()
@@ -338,38 +464,60 @@
         w_out_copy(slot + 1).wait_send()
         w_forward(slot, core).wait_send()
         w_forward(slot, 1 - core).wait_recv()
-
-
-def attention(qkv, w_out, chans):
-    _, heads, head_dim, rows = qkv.shape
+        for c in range(PARTS):
+            acc_copy(c, slot + 1).wait_send()
+        for h in range(2):
+            stat_copy(h, slot + 1).wait_send()
+
+
+def fused(patches, var_embed, agg_query, pos_embed, gain_first, w_qkv, w_out, chans):
+    var_count, rows, d_model = patches.shape
+    columns = w_qkv.shape[1] // 3
+    head_dim = D // HEADS
+    heads = columns // head_dim
     dma = pltpu.SemaphoreType.DMA
     vmem = pl.BlockSpec(memory_space=pltpu.VMEM)
     hbm = pl.BlockSpec(memory_space=pl.ANY)
-    bf16 = jnp.bfloat16
+    bf16, f32 = jnp.bfloat16, jnp.float32
     return pl.pallas_call(
-        functools.partial(attention_kernel, chans, heads),
+        functools.partial(fused_kernel, chans, heads),
         out_shape=(
             jax.ShapeDtypeStruct((chans, heads, head_dim, rows), bf16),
             jax.ShapeDtypeStruct((chans - 1,) + w_out.shape, bf16),
+            jax.ShapeDtypeStruct((rows, d_model), f32),
         ),
-        in_specs=[vmem, hbm],
-        out_specs=(vmem, hbm),
+        in_specs=[hbm, vmem, vmem, hbm, vmem, hbm, hbm],
+        out_specs=(vmem, hbm, vmem),
         scratch_shapes=[
+            pltpu.VMEM(patches.shape, bf16),
+            pltpu.VMEM(w_qkv.shape, bf16),
+            pltpu.VMEM((rows, d_model), bf16),
+            pltpu.VMEM((rows, d_model), f32),
+            pltpu.VMEM((rows, d_model), bf16),
+            pltpu.VMEM((chans - 1, rows, d_model), bf16),
+            pltpu.VMEM((2, 128, rows // 2), f32),
+            pltpu.VMEM((2, chans - 1, 8, rows // 2), f32),
+            pltpu.VMEM((chans - 1, rows // 2, 128), f32),
+            pltpu.VMEM((rows // 2, d_model), bf16),
+            pltpu.VMEM((3, heads, head_dim, rows), bf16),
             pltpu.VMEM((heads, 3, head_dim, rows), bf16),
             pltpu.VMEM((heads, 2, head_dim, rows), bf16),
             pltpu.VMEM((2 * heads, rows, head_dim), bf16),
             pltpu.VMEM((2 * heads, head_dim + 16, rows), bf16),
-            pltpu.VMEM((2 * heads, rows, rows), jnp.float32),
-            pltpu.VMEM((2 * heads, rows, rows), jnp.float32),
+            pltpu.VMEM((2 * heads, rows, rows), f32),
+            pltpu.VMEM((2 * heads, rows, rows), f32),
             pltpu.VMEM((heads, head_dim, rows), bf16),
-            dma, dma((heads,)), dma((heads,)), dma((heads,)), dma((heads,)),
+            dma((PARTS + 2,)),
+            dma((PARTS, chans - 1)), dma((PARTS, chans - 1)),
+            dma((2, chans - 1)), dma((2, chans - 1)),
+            dma((2, heads)), dma((2, heads)), dma((2, heads)), dma((2, heads)),
             dma((heads, chans)), dma((chans, heads)),
             dma((chans - 1,)), dma((chans - 1,)), dma((chans - 1,)), dma((chans - 1,)),
         ],
         compiler_params=pltpu.CompilerParams(
-            collective_id=0, has_side_effects=True, vmem_limit_bytes=48 * 1024 * 1024
+            collective_id=0, has_side_effects=True, vmem_limit_bytes=56 * 1024 * 1024
         ),
-    )(qkv, w_out)
+    )(patches, var_embed, agg_query[None], pos_embed, gain_first[None], w_qkv, w_out)
 
 
 def body_exchange(
@@ -387,33 +535,11 @@
 ):
     var_count, pos_rows, d_model = patches.shape
     chans = lax.axis_size("chan")
-    embedded = patches.astype(jnp.float32) + var_embed[:, None, :]
-    logits = jnp.sum(embedded * agg_query, -1) * (1.0 / math.sqrt(D))
-    local_top = jnp.max(logits, 0)
-    expo_terms = jnp.exp(logits - local_top)
-    part_sum = jnp.sum(expo_terms, 0)
-    part_acc = jnp.sum(expo_terms[:, :, None] * embedded, 0)
-    state = (local_top, part_sum, part_acc)
-    sent = part_acc.astype(jnp.bfloat16)
-    stats = jnp.stack([local_top, part_sum])
-    for turn in range(1, chans):
-        ring = [(i, (i + turn) % chans) for i in range(chans)]
-        there = lax.ppermute(sent, "chan", ring).astype(jnp.float32)
-        there_stats = lax.ppermute(stats, "chan", ring)
-        state = pool_combine(state, (there_stats[0], there_stats[1], there))
-    _, denom_sum, pooled_acc = state
-    resid = pooled_acc / denom_sum[:, None] + pos_embed.astype(jnp.float32)
-    normed = rms_norm(resid, gain_first).astype(jnp.bfloat16)
     columns = w_qkv.shape[2]
-    head_dim = D // HEADS
-    head_count = columns // head_dim
-    factor = jnp.array([math.log2(math.e) / math.sqrt(head_dim), 1.0, 1.0], jnp.float32)
-    qkv = lax.dot_general(
-        w_qkv.reshape(d_model, 3 * columns), normed, (((0,), (1,)), ((), ())),
-        preferred_element_type=jnp.float32,
-    ).reshape(3, head_count, head_dim, pos_rows)
-    qkv = (qkv * factor[:, None, None, None]).astype(jnp.bfloat16)
-    mixed, w_more = attention(qkv, w_out, chans)
+    mixed, w_more, resid = fused(
+        patches, var_embed, agg_query, pos_embed, gain_first,
+        w_qkv.reshape(d_model, 3 * columns), w_out, chans,
+    )
     mixed = mixed.reshape(chans, columns, pos_rows)
     trunk = resid
     for shift in range(chans):

time: 80.2 us -> 74 us (0.923)
  Pallas kernels: 41 us -> 54.1 us
  other arithmetic: 9.29 us -> 0.17 us
  waiting for transfers between devices: 7.94 us -> 0 us
  matrix products: 11.2 us -> 8.29 us
  local copies, waits for them, and re-layouts: 8.79 us -> 10.6 us
  starting transfers between devices: 1.53 us -> 0 us
    pallas_call x1, Pallas kernels: 41 us -> 54.1 us  [fused(): pl.pallas_call(functools.partial(fused_kernel, chans, heads), out_shape=(...]
    ppermute x2 -> x0, waiting for transfers between devices: 7.94 us -> none  [the longest x1 7.94 us: body_exchange(): there = lax.ppermute(sent, 'chan', ring).astype(jnp.float32)]
    reduce_sum x4 -> x0, other arithmetic: 6.49 us -> none  [the longest x1 3.51 us: body_exchange(): logits = jnp.sum(embedded * agg_query, -1) * (1.0 / math.sqrt(D))]
    reshape x0 -> x1, local copies, waits for them, and re-layouts: none -> 4.65 us  [body_exchange(): w_qkv.reshape(d_model, 3 * columns)]
    dot_general x1 -> x0, matrix products: 4.13 us -> none  [body_exchange(): lax.dot_general(w_qkv.reshape(d_model, 3 * columns), normed, (((0,), (1,)...]
    dot_general x1 -> x0, local copies, waits for them, and re-layouts: 3.11 us -> none  [body_exchange(): lax.dot_general(w_qkv.reshape(d_model, 3 * columns), normed, (((0,), (1,)...]
    convert_element_type x2 -> x0, other arithmetic: 2.58 us -> none  [the longest x1 1.71 us: body_exchange(): qkv = (qkv * factor[:, None, None, None]).astype(jnp.bfloat16)]
    ppermute x2 -> x0, starting transfers between devices: 1.53 us -> none  [the longest x1 1.3 us: body_exchange(): there_stats = lax.ppermute(stats, 'chan', ring)]
  transfers between devices with their start and end apart: 2 -> 0, of which waited for: 1 -> 0; matrix products, arithmetic and copies ran while one was open for 9% -> 0% of each run, Pallas kernels for 0% -> 0%
where the time goes in v2:
time: 74 us; the launch traced here: 73.3 us
  Pallas kernels  54.1 us (73%)
  local copies, waits for them, and re-layouts  10.6 us (14%)
  matrix products  8.29 us (11%)
    pallas_call x1, Pallas kernels, fused(): pl.pallas_call(functools.partial(fused_kernel, chans, heads), out_shape=(...  54.1 us
    dot_general x1, matrix products, body_exchange(): jnp.dot(modulated.reshape(var_count * pos_rows, d_model), w_dec, preferre...  6.05 us
    unnamed x13, local copies, waits for them, and re-layouts  4.81 us
    reshape x1, local copies, waits for them, and re-layouts, body_exchange(): w_qkv.reshape(d_model, 3 * columns)  4.65 us
    dot_general x2, matrix products, body_exchange(): lax.dot_general(mixed[shift], w_out if shift == 0 else w_more[shift - 1],...  2.24 us

profile of v2, /device:TPU:11, one launch (start us, length us, event | category | flops | bytes accessed | tf_op | source)
XLA Modules:
  0.0 73.3 jit_solution(17679200800841246806)
XLA Ops:
  0.0 0.0 copy-start
  0.0 4.8 %copy.13 = bf16[1024,3,512]{0,2,1:T(8,128)(2,1)} copy(bf16[1024,3,512]{2,0,1:T(8,128)(2,1)} %param.17) | data formatting | bytes 6291456 | tf_op args[6]
  4.8 4.7 %copy.14.w_qkv_ref = bf16[1024,1536]{1,0:T(8,128)(2,1)} copy(bf16[1024,1536]{0,1:T(8,128)(2,1)} %bitcast.16) | data formatting | bytes 6291456 | tf_op jit(solution)/shard_map/reshape | solution.py:541
  9.4 0.0 copy-start.1
  9.4 54.1 %shard_map.109 = (bf16[2,8,64,256]{3,2,1,0:T(8,128)(2,1)}, bf16[1,512,1024]{2,1,0:T(8,128)(2,1)}, f32[256,1024]{1,0:T(8,128)}) custom-call(bf16[8,256,1024]{2,1,0:T(8,128)(2,1)} %patches_ref.1, f32[8,1024]{1,0:T(8,128)} %embed_ref.1, f32[1,1024]{1,0:T(1,128)} %bitcast.19, bf16[256,1024]{1,0:T(8,128)(2,1)} %pos_ref.1, f32[1,1024]{1,0:T(1,128)} %bitcast.20, ...), custom_call_target="tpu_custom_call" | custom-call | tf_op jit(solution)/shard_map/pallas_call | solution.py:482
  63.6 0.0 copy-start.2
  63.6 0.0 copy-start.4
  63.6 1.2 %fusion.8 = (bf16[1,8,64,256]{3,2,1,0:T(8,128)(2,1)S(1)}, bf16[1,8,64,256]{3,2,1,0:T(8,128)(2,1)S(1)}) fusion(bf16[2,8,64,256]{3,2,1,0:T(8,128)(2,1)} %get-tuple-element.9), kind=kLoop, calls=%fused_computation.15 | loop fusion | bytes 1048576 | tf_op jit(solution)/shard_map/slice | solution.py:547
  64.7 0.0 copy-done.1
  64.8 0.0 copy-start.3
  64.8 0.0 copy-start.5
  64.8 1.7 %convolution_add_fusion.1 = f32[256,1024]{1,0:T(8,128)S(1)} fusion(f32[256,1024]{1,0:T(8,128)} %get-tuple-element.8, bf16[512,256]{1,0:T(8,128)(2,1)S(1)} %bitcast.18, bf16[512,1024]{1,0:T(8,128)(2,1)S(1)} %copy-done.1), kind=kOutput, calls=%fused_computation.8 | convolution fusion | flops 268697600 | bytes 3407872 | tf_op jit(solution)/shard_map/dot_general | solution.py:546
  66.5 0.0 copy-done.2
  66.5 0.5 multiply_reduce_fusion
  67.0 0.0 copy-done.4
  67.1 0.2 fusion.7
  67.2 0.0 copy-done.3
  67.2 0.0 copy-done
  67.3 0.0 copy-done.5
  67.3 6.1 %fusion.4 = bf16[8,256,1024]{2,1,0:T(8,128)(2,1)} fusion(f32[8,1024]{1,0:T(8,128)S(1)} %copy-done.5, f32[8,1024]{1,0:T(8,128)S(1)} %broadcast_add_fusion, f32[256,1024]{1,0:T(8,128)S(1)} %fusion.7, bf16[1024,1024]{1,0:T(8,128)(2,1)S(1)} %copy-done), kind=kOutput, calls=%fused_computation.5 | convolution fusion | flops 4303355904 | bytes 7405568 | tf_op jit(solution)/shard_map/dot_general | solution.py:554
  (2 shorter events, 0.0 us)
Async XLA Ops:
  0.0 67.2 %copy-start = (bf16[1024,1024]{1,0:T(8,128)(2,1)S(1)}, bf16[1024,1024]{1,0:T(8,128)(2,1)}, u32[]{:S(2)}) copy-start(bf16[1024,1024]{1,0:T(8,128)(2,1)} %param.19) | copy-start | bytes 6291460
  9.4 55.3 %copy-start.1 = (bf16[512,1024]{1,0:T(8,128)(2,1)S(1)}, bf16[512,1024]{1,0:T(8,128)(2,1)}, u32[]{:S(2)}) copy-start(bf16[512,1024]{1,0:T(8,128)(2,1)} %w_ref.1) | copy-start | bytes 3145732
  63.6 2.9 %copy-start.2 = (bf16[1,512,1024]{2,1,0:T(8,128)(2,1)S(1)}, bf16[1,512,1024]{2,1,0:T(8,128)(2,1)}, u32[]{:S(2)}) copy-start(bf16[1,512,1024]{2,1,0:T(8,128)(2,1)} %get-tuple-element.10) | copy-start | bytes 3145732
  63.6 3.5 %copy-start.4 = (f32[1024]{0:T(1024)S(1)}, f32[1024]{0:T(1024)}, u32[]{:S(2)}) copy-start(f32[1024]{0:T(1024)} %param.16) | copy-start | bytes 12292
  64.8 2.5 %copy-start.3 = (f32[8,1024]{1,0:T(8,128)S(1)}, f32[8,1024]{1,0:T(8,128)}, u32[]{:S(2)}) copy-start(f32[8,1024]{1,0:T(8,128)} %param.20) | copy-start | bytes 98308
  64.8 2.5 %copy-start.5 = (f32[8,1024]{1,0:T(8,128)S(1)}, f32[8,1024]{1,0:T(8,128)}, u32[]{:S(2)}) copy-start(f32[8,1024]{1,0:T(8,128)} %param.21) | copy-start | bytes 98308

commit v3 on v2

--- a/solution.py
+++ b/solution.py
@@ -340,14 +340,14 @@
         if h == 0:
             load_w.wait()
         for j in range(3):
-            out = jnp.dot(
-                normed[...], w_qkv[:, pl.ds(j * columns, columns)],
+            out = lax.dot_general(
+                w_qkv[pl.ds(j * columns, columns)], normed[...], (((1,), (1,)), ((), ())),
                 preferred_element_type=jnp.float32,
             )
             if j == 0:
                 out = out * (math.log2(math.e) / math.sqrt(head_dim))
             qkv_ref[j, :, :, lanes_of(h)] = (
-                out.T.astype(jnp.bfloat16).reshape(heads, head_dim, half_rows)
+                out.astype(jnp.bfloat16).reshape(heads, head_dim, half_rows)
             )
         for step in range(1, heads):
             block_out(h, step).start()
@@ -472,7 +472,7 @@
 
 def fused(patches, var_embed, agg_query, pos_embed, gain_first, w_qkv, w_out, chans):
     var_count, rows, d_model = patches.shape
-    columns = w_qkv.shape[1] // 3
+    columns = w_qkv.shape[0] // 3
     head_dim = D // HEADS
     heads = columns // head_dim
     dma = pltpu.SemaphoreType.DMA
@@ -538,7 +538,7 @@
     columns = w_qkv.shape[2]
     mixed, w_more, resid = fused(
         patches, var_embed, agg_query, pos_embed, gain_first,
-        w_qkv.reshape(d_model, 3 * columns), w_out, chans,
+        w_qkv.transpose(1, 2, 0).reshape(3 * columns, d_model), w_out, chans,
     )
     mixed = mixed.reshape(chans, columns, pos_rows)
     trunk = resid

time: 74 us -> 69.9 us (0.945)
  local copies, waits for them, and re-layouts: 10.6 us -> 5.97 us
    unnamed x13 -> x12, local copies, waits for them, and re-layouts: 4.81 us -> 0.03 us
    transpose x0 -> x1, local copies, waits for them, and re-layouts: none -> 4.78 us  [body_exchange(): w_qkv.transpose(1, 2, 0).reshape(3 * columns, d_model)]
    reshape x1 -> x0, local copies, waits for them, and re-layouts: 4.65 us -> none  [body_exchange(): w_qkv.reshape(d_model, 3 * columns)]
where the time goes in v3:
time: 69.9 us; the launch traced here: 69.4 us
  Pallas kernels  54.8 us (78%)
  matrix products  8.29 us (12%)
  local copies, waits for them, and re-layouts  5.97 us (9%)
    pallas_call x1, Pallas kernels, fused(): pl.pallas_call(functools.partial(fused_kernel, chans, heads), out_shape=(...  54.8 us
    dot_general x1, matrix products, body_exchange(): jnp.dot(modulated.reshape(var_count * pos_rows, d_model), w_dec, preferre...  6.05 us
    transpose x1, local copies, waits for them, and re-layouts, body_exchange(): w_qkv.transpose(1, 2, 0).reshape(3 * columns, d_model)  4.78 us
    dot_general x2, matrix products, body_exchange(): lax.dot_general(mixed[shift], w_out if shift == 0 else w_more[shift - 1],...  2.24 us

profile of v3, /device:TPU:11, one launch (start us, length us, event | category | flops | bytes accessed | tf_op | source)
XLA Modules:
  0.0 69.4 jit_solution(6442687203959915373)
XLA Ops:
  0.0 0.0 copy-start
  0.0 4.8 %copy.12 = bf16[3,512,1024]{2,1,0:T(8,128)(2,1)} copy(bf16[3,512,1024]{1,2,0:T(8,128)(2,1)} %bitcast.18) | data formatting | bytes 6291456 | tf_op jit(solution)/shard_map/transpose | solution.py:541
  4.8 0.0 copy-start.1
  4.8 54.8 %shard_map.109 = (bf16[2,8,64,256]{3,2,1,0:T(8,128)(2,1)}, bf16[1,512,1024]{2,1,0:T(8,128)(2,1)}, f32[256,1024]{1,0:T(8,128)}) custom-call(bf16[8,256,1024]{2,1,0:T(8,128)(2,1)} %patches_ref.1, f32[8,1024]{1,0:T(8,128)} %embed_ref.1, f32[1,1024]{1,0:T(1,128)} %bitcast.21, bf16[256,1024]{1,0:T(8,128)(2,1)} %pos_ref.1, f32[1,1024]{1,0:T(1,128)} %bitcast.22, ...), custom_call_target="tpu_custom_call" | custom-call | tf_op jit(solution)/shard_map/pallas_call | solution.py:482
  59.6 0.0 copy-start.2
  59.6 0.0 copy-start.4
  59.6 1.2 %fusion.8 = (bf16[1,8,64,256]{3,2,1,0:T(8,128)(2,1)S(1)}, bf16[1,8,64,256]{3,2,1,0:T(8,128)(2,1)S(1)}) fusion(bf16[2,8,64,256]{3,2,1,0:T(8,128)(2,1)} %get-tuple-element.9), kind=kLoop, calls=%fused_computation.15 | loop fusion | bytes 1048576 | tf_op jit(solution)/shard_map/slice | solution.py:547
  60.8 0.0 copy-done.1
  60.8 0.0 copy-start.3
  60.8 0.0 copy-start.5
  60.8 1.7 %convolution_add_fusion.1 = f32[256,1024]{1,0:T(8,128)S(1)} fusion(f32[256,1024]{1,0:T(8,128)} %get-tuple-element.8, bf16[512,256]{1,0:T(8,128)(2,1)S(1)} %bitcast.20, bf16[512,1024]{1,0:T(8,128)(2,1)S(1)} %copy-done.1), kind=kOutput, calls=%fused_computation.8 | convolution fusion | flops 268697600 | bytes 3407872 | tf_op jit(solution)/shard_map/dot_general | solution.py:546
  62.5 0.0 copy-done.2
  62.6 0.5 multiply_reduce_fusion
  63.1 0.0 copy-done.4
  63.1 0.2 fusion.7
  63.3 0.0 copy-done.3
  63.3 0.0 copy-done
  63.3 0.0 copy-done.5
  63.3 6.1 %fusion.4 = bf16[8,256,1024]{2,1,0:T(8,128)(2,1)} fusion(f32[8,1024]{1,0:T(8,128)S(1)} %copy-done.5, f32[8,1024]{1,0:T(8,128)S(1)} %broadcast_add_fusion, f32[256,1024]{1,0:T(8,128)S(1)} %fusion.7, bf16[1024,1024]{1,0:T(8,128)(2,1)S(1)} %copy-done), kind=kOutput, calls=%fused_computation.5 | convolution fusion | flops 4303355904 | bytes 7405568 | tf_op jit(solution)/shard_map/dot_general | solution.py:554
  (2 shorter events, 0.0 us)
Async XLA Ops:
  0.0 63.3 %copy-start = (bf16[1024,1024]{1,0:T(8,128)(2,1)S(1)}, bf16[1024,1024]{1,0:T(8,128)(2,1)}, u32[]{:S(2)}) copy-start(bf16[1024,1024]{1,0:T(8,128)(2,1)} %param.19) | copy-start | bytes 6291460
  4.8 56.0 %copy-start.1 = (bf16[512,1024]{1,0:T(8,128)(2,1)S(1)}, bf16[512,1024]{1,0:T(8,128)(2,1)}, u32[]{:S(2)}) copy-start(bf16[512,1024]{1,0:T(8,128)(2,1)} %w_ref.1) | copy-start | bytes 3145732
  59.6 2.9 %copy-start.2 = (bf16[1,512,1024]{2,1,0:T(8,128)(2,1)S(1)}, bf16[1,512,1024]{2,1,0:T(8,128)(2,1)}, u32[]{:S(2)}) copy-start(bf16[1,512,1024]{2,1,0:T(8,128)(2,1)} %get-tuple-element.10) | copy-start | bytes 3145732
  59.6 3.5 %copy-start.4 = (f32[1024]{0:T(1024)S(1)}, f32[1024]{0:T(1024)}, u32[]{:S(2)}) copy-start(f32[1024]{0:T(1024)} %param.16) | copy-start | bytes 12292
  60.8 2.5 %copy-start.3 = (f32[8,1024]{1,0:T(8,128)S(1)}, f32[8,1024]{1,0:T(8,128)}, u32[]{:S(2)}) copy-start(f32[8,1024]{1,0:T(8,128)} %param.20) | copy-start | bytes 98308
  60.8 2.5 %copy-start.5 = (f32[8,1024]{1,0:T(8,128)S(1)}, f32[8,1024]{1,0:T(8,128)}, u32[]{:S(2)}) copy-start(f32[8,1024]{1,0:T(8,128)} %param.21) | copy-start | bytes 98308

commit v4 on v3

--- a/solution.py
+++ b/solution.py
@@ -160,7 +160,7 @@
     got, part, k_rows, v_cols, score_a, score_b, stage,
     load_sem, acc_send, acc_recv, stat_send, stat_recv,
     send_sem, recv_sem, fwd_send, fwd_recv, out_send, out_recv,
-    w_send, w_recv, w_fsend, w_frecv,
+    w_send, w_recv, w_fsend, w_frecv, pass_send,
 ):
     space = lax.axis_index("space")
     chan = lax.axis_index("chan")
@@ -193,7 +193,7 @@
     count = 0
     for step in range(heads):
         for turn in range(chans):
-            if step == 0 and turn == 0:
+            if (step == 0) == (turn == 0):
                 continue
             pl.semaphore_signal(
                 barrier, inc=1,
@@ -392,6 +392,20 @@
             device_id={"space": partner}, device_id_type=MESH,
         )
 
+    def pass_on(origin, turn):
+        return pltpu.make_async_remote_copy(
+            src_ref=mixed_ref.at[0, origin], dst_ref=mixed_ref.at[(chans - turn) % chans, origin],
+            send_sem=pass_send.at[origin, turn - 1],
+            recv_sem=out_recv.at[(chans - turn) % chans, origin],
+            device_id={"chan": lax.rem(chan + turn, chans)}, device_id_type=MESH,
+        )
+
+    def relay(step):
+        origin = lax.rem(chip + heads - step, heads)
+        out_wait(0, origin).wait_recv()
+        for turn in range(1, chans):
+            pass_on(origin, turn).start()
+
     def first_pass(step, scores):
         query = got[same_core(step), 0]
 
@@ -424,13 +438,13 @@
         @pl.when(step == 0)
         def _():
             mixed_ref[0, chip] = result
+            for turn in range(1, chans):
+                out_copy(step, turn).start()
 
         @pl.when(step != 0)
         def _():
             out_copy(step, 0).start()
 
-        for turn in range(1, chans):
-            out_copy(step, turn).start()
         return jnp.max(top, 0, keepdims=True)
 
     one = first_pass(0, score_a)
@@ -441,7 +455,17 @@
 
     def pair(i, top):
         top = both(2 * i, score_a, top, score_b)
-        return both(2 * i + 1, score_b, top, score_a)
+        top = both(2 * i + 1, score_b, top, score_a)
+
+        @pl.when(i > 1)
+        def _():
+            relay(2 * i - 2)
+
+        @pl.when(i > 0)
+        def _():
+            relay(2 * i - 1)
+
+        return top
 
     top = lax.fori_loop(0, heads // 4, pair, top)
     for slot in range(chans - 1):
@@ -449,16 +473,20 @@
         w_forward(slot, core).start()
     lax.fori_loop(heads // 4, heads // 2, pair, top)
 
+    for step in range(heads - 2, heads):
+        relay(step)
     for step in range(1, heads):
         for h in range(2):
             block_out(h, step).wait_send()
         out_copy(step, 0).wait_send()
-        out_wait(0, same_core(step)).wait_recv()
     for step in range(heads):
         for h in range(2):
             forward(h, step).wait_send()
         for turn in range(1, chans):
-            out_copy(step, turn).wait_send()
+            if step == 0:
+                out_copy(step, turn).wait_send()
+            else:
+                pass_on(same_core(step), turn).wait_send()
             out_wait(turn, step).wait_recv()
     for slot in range(chans - 1):
         w_out_copy(slot + 1).wait_send()
@@ -513,6 +541,7 @@
             dma((2, heads)), dma((2, heads)), dma((2, heads)), dma((2, heads)),
             dma((heads, chans)), dma((chans, heads)),
             dma((chans - 1,)), dma((chans - 1,)), dma((chans - 1,)), dma((chans - 1,)),
+            dma((heads, chans - 1)),
         ],
         compiler_params=pltpu.CompilerParams(
             collective_id=0, has_side_effects=True, vmem_limit_bytes=56 * 1024 * 1024

time: 69.9 us -> 70.2 us (level)
  the two profiles are of different devices: /device:TPU:11 before, /device:TPU:0 now
where the time goes in v4:
time: 70.2 us; the launch traced here: 70 us
  Pallas kernels  55.4 us (79%)
  matrix products  8.3 us (12%)
  local copies, waits for them, and re-layouts  5.97 us (9%)
    pallas_call x1, Pallas kernels, fused(): pl.pallas_call(functools.partial(fused_kernel, chans, heads), out_shape=(...  55.4 us
    dot_general x1, matrix products, body_exchange(): jnp.dot(modulated.reshape(var_count * pos_rows, d_model), w_dec, preferre...  6.05 us
    transpose x1, local copies, waits for them, and re-layouts, body_exchange(): w_qkv.transpose(1, 2, 0).reshape(3 * columns, d_model)  4.78 us
    dot_general x2, matrix products, body_exchange(): lax.dot_general(mixed[shift], w_out if shift == 0 else w_more[shift - 1],...  2.25 us

profile of v4, /device:TPU:0, one launch (start us, length us, event | category | flops | bytes accessed | tf_op | source)
XLA Modules:
  0.0 70.0 jit_solution(14953697488379631022)
XLA Ops:
  0.0 0.0 copy-start
  0.0 4.8 %copy.12 = bf16[3,512,1024]{2,1,0:T(8,128)(2,1)} copy(bf16[3,512,1024]{1,2,0:T(8,128)(2,1)} %bitcast.18) | data formatting | bytes 6291456 | tf_op jit(solution)/shard_map/transpose | solution.py:570
  4.8 0.0 copy-start.1
  4.8 55.4 %shard_map.109 = (bf16[2,8,64,256]{3,2,1,0:T(8,128)(2,1)}, bf16[1,512,1024]{2,1,0:T(8,128)(2,1)}, f32[256,1024]{1,0:T(8,128)}) custom-call(bf16[8,256,1024]{2,1,0:T(8,128)(2,1)} %patches_ref.1, f32[8,1024]{1,0:T(8,128)} %embed_ref.1, f32[1,1024]{1,0:T(1,128)} %bitcast.21, bf16[256,1024]{1,0:T(8,128)(2,1)} %pos_ref.1, f32[1,1024]{1,0:T(1,128)} %bitcast.22, ...), custom_call_target="tpu_custom_call" | custom-call | tf_op jit(solution)/shard_map/pallas_call | solution.py:510
  60.2 0.0 copy-start.2
  60.2 0.0 copy-start.4
  60.3 1.2 %fusion.8 = (bf16[1,8,64,256]{3,2,1,0:T(8,128)(2,1)S(1)}, bf16[1,8,64,256]{3,2,1,0:T(8,128)(2,1)S(1)}) fusion(bf16[2,8,64,256]{3,2,1,0:T(8,128)(2,1)} %get-tuple-element.9), kind=kLoop, calls=%fused_computation.15 | loop fusion | bytes 1048576 | tf_op jit(solution)/shard_map/slice | solution.py:576
  61.4 0.0 copy-done.1
  61.4 0.0 copy-start.3
  61.4 0.0 copy-start.5
  61.4 1.7 %convolution_add_fusion.1 = f32[256,1024]{1,0:T(8,128)S(1)} fusion(f32[256,1024]{1,0:T(8,128)} %get-tuple-element.8, bf16[512,256]{1,0:T(8,128)(2,1)S(1)} %bitcast.20, bf16[512,1024]{1,0:T(8,128)(2,1)S(1)} %copy-done.1), kind=kOutput, calls=%fused_computation.8 | convolution fusion | flops 268697600 | bytes 3407872 | tf_op jit(solution)/shard_map/dot_general | solution.py:575
  63.2 0.0 copy-done.2
  63.2 0.6 multiply_reduce_fusion
  63.7 0.0 copy-done.4
  63.7 0.2 fusion.7
  63.9 0.0 copy-done.3
  63.9 0.0 copy-done
  63.9 0.0 copy-done.5
  63.9 6.1 %fusion.4 = bf16[8,256,1024]{2,1,0:T(8,128)(2,1)} fusion(f32[8,1024]{1,0:T(8,128)S(1)} %copy-done.5, f32[8,1024]{1,0:T(8,128)S(1)} %broadcast_add_fusion, f32[256,1024]{1,0:T(8,128)S(1)} %fusion.7, bf16[1024,1024]{1,0:T(8,128)(2,1)S(1)} %copy-done), kind=kOutput, calls=%fused_computation.5 | convolution fusion | flops 4303355904 | bytes 7405568 | tf_op jit(solution)/shard_map/dot_general | solution.py:583
  (2 shorter events, 0.0 us)
Async XLA Ops:
  0.0 63.9 %copy-start = (bf16[1024,1024]{1,0:T(8,128)(2,1)S(1)}, bf16[1024,1024]{1,0:T(8,128)(2,1)}, u32[]{:S(2)}) copy-start(bf16[1024,1024]{1,0:T(8,128)(2,1)} %param.19) | copy-start | bytes 6291460
  4.8 56.6 %copy-start.1 = (bf16[512,1024]{1,0:T(8,128)(2,1)S(1)}, bf16[512,1024]{1,0:T(8,128)(2,1)}, u32[]{:S(2)}) copy-start(bf16[512,1024]{1,0:T(8,128)(2,1)} %w_ref.1) | copy-start | bytes 3145732
  60.2 2.9 %copy-start.2 = (bf16[1,512,1024]{2,1,0:T(8,128)(2,1)S(1)}, bf16[1,512,1024]{2,1,0:T(8,128)(2,1)}, u32[]{:S(2)}) copy-start(bf16[1,512,1024]{2,1,0:T(8,128)(2,1)} %get-tuple-element.10) | copy-start | bytes 3145732
  60.2 3.5 %copy-start.4 = (f32[1024]{0:T(1024)S(1)}, f32[1024]{0:T(1024)}, u32[]{:S(2)}) copy-start(f32[1024]{0:T(1024)} %param.16) | copy-start | bytes 12292
  61.4 2.5 %copy-start.3 = (f32[8,1024]{1,0:T(8,128)S(1)}, f32[8,1024]{1,0:T(8,128)}, u32[]{:S(2)}) copy-start(f32[8,1024]{1,0:T(8,128)} %param.20) | copy-start | bytes 98308
  61.4 2.5 %copy-start.5 = (f32[8,1024]{1,0:T(8,128)S(1)}, f32[8,1024]{1,0:T(8,128)}, u32[]{:S(2)}) copy-start(f32[8,1024]{1,0:T(8,128)} %param.21) | copy-start | bytes 98308

commit v5 on v3

--- a/solution.py
+++ b/solution.py
@@ -349,7 +349,7 @@
             qkv_ref[j, :, :, lanes_of(h)] = (
                 out.astype(jnp.bfloat16).reshape(heads, head_dim, half_rows)
             )
-        for step in range(1, heads):
+        for step in sorted(range(1, heads), key=lambda k: -min(k, heads - k)):
             block_out(h, step).start()
         got[chip, :, :, lanes_of(h)] = qkv_ref[:, chip, :, lanes_of(h)]
         forward(h, chip).start()
@@ -359,8 +359,7 @@
         w_out_copy(turn).start()
 
     for h in range(2):
-        @pl.loop(1, heads)
-        def _(step):
+        for step in sorted(range(1, heads), key=lambda k: -min(k, heads - k)):
             origin = lax.rem(chip + heads - step, heads)
             block_in(h, origin).wait_recv()
             forward(h, origin).start()

time: 69.9 us -> 70.1 us (level)
  no operation moved by 1% of the time
where the time goes in v5:
time: 70.1 us; the launch traced here: 69.9 us
  Pallas kernels  55.3 us (79%)
  matrix products  8.29 us (12%)
  local copies, waits for them, and re-layouts  5.97 us (9%)
    pallas_call x1, Pallas kernels, fused(): pl.pallas_call(functools.partial(fused_kernel, chans, heads), out_shape=(...  55.3 us
    dot_general x1, matrix products, body_exchange(): jnp.dot(modulated.reshape(var_count * pos_rows, d_model), w_dec, preferre...  6.06 us
    transpose x1, local copies, waits for them, and re-layouts, body_exchange(): w_qkv.transpose(1, 2, 0).reshape(3 * columns, d_model)  4.78 us
    dot_general x2, matrix products, body_exchange(): lax.dot_general(mixed[shift], w_out if shift == 0 else w_more[shift - 1],...  2.24 us

profile of v5, /device:TPU:11, one launch (start us, length us, event | category | flops | bytes accessed | tf_op | source)
XLA Modules:
  0.0 69.9 jit_solution(13309647393943269428)
XLA Ops:
  0.0 0.0 copy-start
  0.0 4.8 %copy.12 = bf16[3,512,1024]{2,1,0:T(8,128)(2,1)} copy(bf16[3,512,1024]{1,2,0:T(8,128)(2,1)} %bitcast.18) | data formatting | bytes 6291456 | tf_op jit(solution)/shard_map/transpose | solution.py:540
  4.8 0.0 copy-start.1
  4.8 55.3 %shard_map.109 = (bf16[2,8,64,256]{3,2,1,0:T(8,128)(2,1)}, bf16[1,512,1024]{2,1,0:T(8,128)(2,1)}, f32[256,1024]{1,0:T(8,128)}) custom-call(bf16[8,256,1024]{2,1,0:T(8,128)(2,1)} %patches_ref.1, f32[8,1024]{1,0:T(8,128)} %embed_ref.1, f32[1,1024]{1,0:T(1,128)} %bitcast.21, bf16[256,1024]{1,0:T(8,128)(2,1)} %pos_ref.1, f32[1,1024]{1,0:T(1,128)} %bitcast.22, ...), custom_call_target="tpu_custom_call" | custom-call | tf_op jit(solution)/shard_map/pallas_call | solution.py:481
  60.1 0.0 copy-start.2
  60.1 0.0 copy-start.4
  60.1 1.2 %fusion.8 = (bf16[1,8,64,256]{3,2,1,0:T(8,128)(2,1)S(1)}, bf16[1,8,64,256]{3,2,1,0:T(8,128)(2,1)S(1)}) fusion(bf16[2,8,64,256]{3,2,1,0:T(8,128)(2,1)} %get-tuple-element.9), kind=kLoop, calls=%fused_computation.15 | loop fusion | bytes 1048576 | tf_op jit(solution)/shard_map/slice | solution.py:546
  61.3 0.0 copy-done.1
  61.3 0.0 copy-start.3
  61.3 0.0 copy-start.5
  61.3 1.7 %convolution_add_fusion.1 = f32[256,1024]{1,0:T(8,128)S(1)} fusion(f32[256,1024]{1,0:T(8,128)} %get-tuple-element.8, bf16[512,256]{1,0:T(8,128)(2,1)S(1)} %bitcast.20, bf16[512,1024]{1,0:T(8,128)(2,1)S(1)} %copy-done.1), kind=kOutput, calls=%fused_computation.8 | convolution fusion | flops 268697600 | bytes 3407872 | tf_op jit(solution)/shard_map/dot_general | solution.py:545
  63.0 0.0 copy-done.2
  63.0 0.5 multiply_reduce_fusion
  63.6 0.0 copy-done.4
  63.6 0.2 fusion.7
  63.8 0.0 copy-done.3
  63.8 0.0 copy-done
  63.8 0.0 copy-done.5
  63.8 6.1 %fusion.4 = bf16[8,256,1024]{2,1,0:T(8,128)(2,1)} fusion(f32[8,1024]{1,0:T(8,128)S(1)} %copy-done.5, f32[8,1024]{1,0:T(8,128)S(1)} %broadcast_add_fusion, f32[256,1024]{1,0:T(8,128)S(1)} %fusion.7, bf16[1024,1024]{1,0:T(8,128)(2,1)S(1)} %copy-done), kind=kOutput, calls=%fused_computation.5 | convolution fusion | flops 4303355904 | bytes 7405568 | tf_op jit(solution)/shard_map/dot_general | solution.py:553
  (2 shorter events, 0.0 us)
Async XLA Ops:
  0.0 63.8 %copy-start = (bf16[1024,1024]{1,0:T(8,128)(2,1)S(1)}, bf16[1024,1024]{1,0:T(8,128)(2,1)}, u32[]{:S(2)}) copy-start(bf16[1024,1024]{1,0:T(8,128)(2,1)} %param.19) | copy-start | bytes 6291460
  4.8 56.5 %copy-start.1 = (bf16[512,1024]{1,0:T(8,128)(2,1)S(1)}, bf16[512,1024]{1,0:T(8,128)(2,1)}, u32[]{:S(2)}) copy-start(bf16[512,1024]{1,0:T(8,128)(2,1)} %w_ref.1) | copy-start | bytes 3145732
  60.1 2.9 %copy-start.2 = (bf16[1,512,1024]{2,1,0:T(8,128)(2,1)S(1)}, bf16[1,512,1024]{2,1,0:T(8,128)(2,1)}, u32[]{:S(2)}) copy-start(bf16[1,512,1024]{2,1,0:T(8,128)(2,1)} %get-tuple-element.10) | copy-start | bytes 3145732
  60.1 3.5 %copy-start.4 = (f32[1024]{0:T(1024)S(1)}, f32[1024]{0:T(1024)}, u32[]{:S(2)}) copy-start(f32[1024]{0:T(1024)} %param.16) | copy-start | bytes 12292
  61.3 2.5 %copy-start.3 = (f32[8,1024]{1,0:T(8,128)S(1)}, f32[8,1024]{1,0:T(8,128)}, u32[]{:S(2)}) copy-start(f32[8,1024]{1,0:T(8,128)} %param.20) | copy-start | bytes 98308
  61.3 2.5 %copy-start.5 = (f32[8,1024]{1,0:T(8,128)S(1)}, f32[8,1024]{1,0:T(8,128)}, u32[]{:S(2)}) copy-start(f32[8,1024]{1,0:T(8,128)} %param.21) | copy-start | bytes 98308
